TPU v7x, 256 devices: a whole 4x4x8 slice. The times are simulated.
256 devices in a mesh: seq: 32 (over x_lo, z, core), tp: 8 (over y, x_hi).
Axes of the slice: x: 4 (x_hi: 2, x_lo: 2; x = x_hi * 2 + x_lo), y: 4, z: 8, core: 2. Of those that a mesh axis runs over, the one named last changes fastest.
Arguments:
- values: bfloat16 [8192, 4096], P('seq', 'tp'), may hold values from -6 to 6
- gate: bfloat16 [8192, 4096], P('seq', 'tp'), may hold values from -6 to 6
- out_grad: bfloat16 [8192, 4096], P('seq', 'tp'), may hold values from -6 to 6
- out_weight: bfloat16 [4096, 4096], P(None, 'tp'), may hold values from -0.09375 to 0.09375
- filt: float32 [8192, 4096], P('seq', 'tp'), may hold values from -6 to 6
- decay: float32 [4096], P('tp'), may hold values from 0.5 to 16
Outputs:
- d_values: bfloat16 [8192, 4096], P('seq', 'tp')
- d_gate: bfloat16 [8192, 4096], P('seq', 'tp')
- d_filt: float32 [8192, 4096], P('seq', 'tp')
- decay_grad: float32 [4096], P('tp')
- d_out_weight: float32 [4096, 4096], P('seq', 'tp')
All inputs are finite; a program needn't handle non-finite values.
Results may differ from a plain program's by a relative error of at most 0.0085.
Values may be sent and summed in bfloat16 or wider, within the bound.
A program may use at most 128 MiB of HBM per device.

v0:
```python
import math

import jax
import jax.numpy as jnp
from jax import lax
from jax.sharding import PartitionSpec as P

HIGHEST = lax.Precision.HIGHEST
TWO_PI = 2.0 * math.pi


def angles(left, right, modulus):
    index = left[:, None] * right[None, :] % modulus
    phase = index.astype(jnp.float32) * (TWO_PI / modulus)
    return jnp.cos(phase), jnp.sin(phase)


def to_channels(block, parts):
    lead = block.shape[:-2]
    tok_rows, width = block.shape[-2:]
    nd = len(lead)
    split = block.reshape(lead + (tok_rows, parts, width // parts))
    split = jnp.transpose(split, tuple(range(nd)) + (nd + 1, nd + 2, nd))
    return lax.all_to_all(split, "seq", split_axis=nd, concat_axis=nd, tiled=True)


def to_tokens(block, parts):
    lead = block.shape[:-3]
    _, sub, tok_rows = block.shape[-3:]
    nd = len(lead)
    moved = lax.all_to_all(block, "seq", split_axis=nd, concat_axis=nd, tiled=True)
    moved = moved.reshape(lead + (parts * sub, tok_rows))
    return jnp.transpose(moved, tuple(range(nd)) + (nd + 1, nd))


class Dft:
    def __init__(self, parts, rows):
        outer = 2 * parts
        self.n = outer * rows
        self.rows = rows
        p_idx = jnp.arange(parts, dtype=jnp.int32)
        k1_idx = jnp.arange(outer, dtype=jnp.int32)
        r_idx = jnp.arange(rows, dtype=jnp.int32)
        c1, s1 = angles(k1_idx, p_idx, outer)
        self.fwd_outer = jnp.concatenate([c1, -s1], axis=0)
        self.inv_outer = jnp.concatenate([c1.T, -s1.T], axis=1) / self.n
        self.twid_c, self.twid_s = angles(k1_idx, r_idx, self.n)
        gc, gs = angles(r_idx, r_idx, rows)
        self.fwd_inner = jnp.concatenate(
            [jnp.concatenate([gc, -gs], axis=1), jnp.concatenate([gs, gc], axis=1)], axis=0
        )
        self.inv_inner = jnp.concatenate(
            [jnp.concatenate([gc, gs], axis=1), jnp.concatenate([-gs, gc], axis=1)], axis=0
        )

    def forward(self, x):
        y = jnp.einsum("kp,fpcr->fkcr", self.fwd_outer, x, precision=HIGHEST)
        outer = self.fwd_outer.shape[0] // 2
        yr, yi = y[:, :outer], y[:, outer:]
        tc = self.twid_c[None, :, None, :]
        ts = self.twid_s[None, :, None, :]
        zr = yr * tc + yi * ts
        zi = yi * tc - yr * ts
        z = jnp.concatenate([zr, zi], axis=-1)
        out = jnp.einsum("fkcr,rq->fkcq", z, self.fwd_inner, precision=HIGHEST)
        return out[..., : self.rows], out[..., self.rows :]

    def inverse_real(self, zr, zi):
        z = jnp.concatenate([zr, zi], axis=-1)
        u = jnp.einsum("fkcq,qr->fkcr", z, self.inv_inner, precision=HIGHEST)
        ur, ui = u[..., : self.rows], u[..., self.rows :]
        tc = self.twid_c[None, :, None, :]
        ts = self.twid_s[None, :, None, :]
        vr = ur * tc - ui * ts
        vi = ur * ts + ui * tc
        v = jnp.concatenate([vr, vi], axis=1)
        return jnp.einsum("pk,fkcr->fpcr", self.inv_outer, v, precision=HIGHEST)


def pair_products(full_grad, gated_home, core):
    half = gated_home.shape[1] // 2
    keep_cols = lax.dynamic_slice_in_dim(gated_home, core * half, half, axis=1)
    send_cols = lax.dynamic_slice_in_dim(gated_home, (1 - core) * half, half, axis=1)
    dims = (((0,), (0,)), ((), ()))
    keep = lax.dot_general(full_grad, keep_cols, dims, preferred_element_type=jnp.float32)
    send = lax.dot_general(full_grad, send_cols, dims, preferred_element_type=jnp.float32)
    return keep, send


def pair_reduce(keep, send, core, parts, norm_scale):
    pairs = [(i, i ^ 1) for i in range(parts)]
    groups = [list(range(0, parts, 2)), list(range(1, parts, 2))]
    pair_sum = (keep + lax.ppermute(send, "seq", pairs)) * norm_scale
    rows = lax.psum_scatter(pair_sum, "seq", scatter_dimension=0, tiled=True, axis_index_groups=groups)
    block = rows.shape[0] // 2
    own = lax.dynamic_slice_in_dim(rows, core * block, block, axis=0)
    given = lax.dynamic_slice_in_dim(rows, (1 - core) * block, block, axis=0)
    got = lax.ppermute(given, "seq", pairs)
    return jnp.where(core == 0, jnp.concatenate([own, got], axis=1), jnp.concatenate([got, own], axis=1))

def on_device(values, gate, out_grad, out_weight, filt, decay):
    tok_rows, width = values.shape
    parts = lax.axis_size("seq")
    my_index = lax.axis_index("seq")
    sub = width // parts
    length = tok_rows * parts
    norm_scale = 1.0 / math.sqrt(length)

    early = to_channels(jnp.stack([values.astype(jnp.float32), filt]), parts)
    filt_c = early[1]
    gate_c = to_channels(gate, parts).astype(jnp.float32)

    full_grad = lax.all_gather(out_grad, "tp", axis=1, tiled=True)
    grad_y = jnp.dot(full_grad, out_weight, preferred_element_type=jnp.float32).astype(jnp.bfloat16)

    values_c = early[0]

    my_decay = lax.dynamic_slice_in_dim(decay, my_index * sub, sub)
    tok = (
        jnp.arange(parts, dtype=jnp.int32)[:, None, None] * tok_rows
        + jnp.arange(tok_rows, dtype=jnp.int32)[None, None, :]
    )
    position = tok.astype(jnp.float32) / length
    window = jnp.exp(-my_decay[None, :, None] * position)
    kernel = filt_c * window * norm_scale

    dft = Dft(parts, tok_rows)
    vk_r, vk_i = dft.forward(jnp.stack([values_c, kernel]))
    v_r, k_r = vk_r[0], vk_r[1]
    v_i, k_i = vk_i[0], vk_i[1]
    conv_out = dft.inverse_real((v_r * k_r - v_i * k_i)[None], (v_r * k_i + v_i * k_r)[None])[0]
    gated_out = (gate_c * conv_out).astype(jnp.bfloat16)
    gated_home = to_tokens(gated_out, parts)
    core = my_index % 2
    keep, send, grad_y = lax.optimization_barrier(pair_products(full_grad, gated_home, core) + (grad_y,))
    d_out_weight = pair_reduce(keep, send, core, parts, norm_scale)

    grad_c = to_channels(grad_y, parts).astype(jnp.float32)
    gated_grad = grad_c * gate_c
    g_r, g_i = dft.forward(gated_grad[None])
    g_r, g_i = g_r[0], g_i[0]
    prod_r = jnp.stack([k_r * g_r + k_i * g_i, v_r * g_r + v_i * g_i])
    prod_i = jnp.stack([k_r * g_i - k_i * g_r, v_r * g_i - v_i * g_r])
    conv = dft.inverse_real(prod_r, prod_i)
    conv_grad, kernel_grad = conv[0], conv[1]

    d_values = conv_grad.astype(jnp.bfloat16)
    d_gate = (grad_c * conv_out).astype(jnp.bfloat16)
    d_filt_c = kernel_grad * window * norm_scale
    decay_part = jnp.sum(position * kernel_grad * kernel, axis=(0, 2))

    back = to_tokens(jnp.stack([d_values, d_gate]), parts)
    d_filt = to_tokens(d_filt_c, parts)
    spread = jnp.broadcast_to(decay_part[None, :], (parts, sub))
    gathered = lax.all_to_all(spread, "seq", split_axis=0, concat_axis=0, tiled=True)
    decay_grad = -norm_scale * gathered.reshape(width)
    return (back[0], back[1], d_filt, decay_grad, d_out_weight)


def solution(mesh):
    in_specs = (
        P("seq", "tp"),
        P("seq", "tp"),
        P("seq", "tp"),
        P(None, "tp"),
        P("seq", "tp"),
        P("tp"),
    )
    out_specs = (P("seq", "tp"), P("seq", "tp"), P("seq", "tp"), P("tp"), P("seq", "tp"))
    return jax.shard_map(
        on_device, mesh=mesh, in_specs=in_specs, out_specs=out_specs, check_vma=False
    )
```

profile of v0, /device:TPU:1, one launch (start us, length us, event | category | flops | bytes accessed | tf_op | source)
XLA Modules:
  0.0 230.2 jit_solution(8854696864315791053)
XLA Ops:
  7.2 1.1 copy.37
  8.3 1.2 copy.38
  9.6 1.1 copy.39
  10.7 11.0 %all-to-all-start = ((f32[2,32,16,256]{3,2,0,1:T(8,128)}), f32[2,32,16,256]{3,2,0,1:T(8,128)S(1)}, u32[]{:S(2)}, u32[]{:S(2)}) async-start(f32[2,32,16,256]{3,2,0,1:T(8,128)} %copy.39), calls=%async_computation | async-start | bytes 2097152 | tf_op jit(solution)/shard_map/all_to_all | solution.py:24
  22.5 0.8 copy.43
  23.4 0.8 dynamic-slice_negate_fusion
  24.2 0.7 sine_negate_fusion
  25.2 1.0 fusion.56
  26.2 1.0 fusion.54
  27.3 20.9 %all-to-all-done = f32[2,32,16,256]{3,2,0,1:T(8,128)S(1)} async-done(((f32[2,32,16,256]{3,2,0,1:T(8,128)}), f32[2,32,16,256]{3,2,0,1:T(8,128)S(1)}, u32[]{:S(2)}, u32[]{:S(2)}) %all-to-all-start) | async-done | bytes 1048608 | tf_op jit(solution)/shard_map/all_to_all | solution.py:24
  48.3 6.5 %all-to-all-start.1 = ((bf16[32,16,256]{2,1,0:T(8,128)(2,1)}), bf16[32,16,256]{2,1,0:T(8,128)(2,1)}, u32[]{:S(2)}, u32[]{:S(2)}) async-start(bf16[32,16,256]{2,1,0:T(8,128)(2,1)} %bitcast.9), calls=%async_computation.1 | async-start | bytes 524288 | tf_op jit(solution)/shard_map/all_to_all | solution.py:24
  55.5 3.6 %convolution_bitcast_fusion.2 = f32[2,128,16,256]{3,1,2,0:T(8,128)S(1)} fusion(f32[1,32,16,256]{3,1,2,0:T(8,128)S(1)} %multiply_multiply_fusion.1, f32[1,32,16,256]{3,1,2,0:T(8,128)S(1)} %copy.65, f32[64,32]{0,1:T(8,128)S(1)} %get-tuple-element.50, f32[64,32]{0,1:T(8,128)S(1)} %get-tuple-element.51), kind=kOutput, calls=%fused_computation.13 | convolution fusion | flops 402919424 | bytes 5259264 | tf_op jit(solution)/shard_map/kp,fpcr->fkcr/dot_general | solution.py:57
  60.2 9.7 %fusion.6 = f32[2,64,16,512]{3,2,1,0:T(8,128)S(1)} fusion(f32[2,64,16,512]{3,1,2,0:T(8,128)S(1)} %pad_maximum_fusion, f32[256,256]{1,0:T(8,128)S(1)} %get-tuple-element.55, f32[256,256]{1,0:T(8,128)S(1)} %get-tuple-element.54, f32[256,256]{1,0:T(8,128)S(1)} %fusion.56), kind=kOutput, calls=%fused_computation.10 | convolution fusion | flops 6443237376 | bytes 9175040 | tf_op jit(solution)/shard_map/fkcr,rq->fkcq/dot_general | solution.py:65
  70.3 1.6 copy-done
  72.0 3.5 %fusion.17 = f32[1,64,16,512]{3,2,1,0:T(8,128)S(1)} fusion(f32[1,64,16,256]{3,2,1,0:T(8,128)S(1)} %get-tuple-element.35, f32[1,64,16,256]{3,2,1,0:T(8,128)S(1)} %get-tuple-element.34, f32[256,256]{1,0:T(8,128)S(1)} %get-tuple-element.55, f32[256,256]{1,0:T(8,128)S(1)} %fusion.56, f32[256,256]{1,0:T(8,128)S(1)} %get-tuple-element.54), kind=kOutput, calls=%fused_computation.31 | convolution fusion | flops 3222536192 | bytes 4980736 | tf_op jit(solution)/shard_map/fkcq,qr->fkcr/dot_general | solution.py:70
  76.0 4.2 %fusion.37 = (bf16[32,16,256]{2,0,1:T(8,128)(2,1)S(1)}, f32[32,16,256]{2,0,1:T(8,128)}) fusion(bf16[32,16,256]{2,1,0:T(8,128)(2,1)} %all-to-all-done.1, f32[32,64]{1,0:T(8,128)} %get-tuple-element.56, f32[32,64]{1,0:T(8,128)} %get-tuple-element.57, f32[128,16,256]{2,1,0:T(8,128)S(1)} %maximum_bitcast_fusion.2), kind=kOutput, calls=%fused_computation.62 | convolution fusion | flops 201728000 | bytes 3162112 | tf_op jit(solution)/shard_map/pk,fkcr->fpcr/dot_general | solution.py:77
  80.2 0.9 copy.46
  81.1 8.4 %all-to-all-start.2 = ((bf16[32,16,256]{2,1,0:T(8,128)(2,1)}), bf16[32,16,256]{2,1,0:T(8,128)(2,1)S(1)}, u32[]{:S(2)}, u32[]{:S(2)}) async-start(bf16[32,16,256]{2,1,0:T(8,128)(2,1)} %copy.46), calls=%async_computation.2 | async-start | bytes 524288 | tf_op jit(solution)/shard_map/all_to_all | solution.py:31
  89.6 11.8 %all-to-all-done.2 = bf16[32,16,256]{2,1,0:T(8,128)(2,1)S(1)} async-done(((bf16[32,16,256]{2,1,0:T(8,128)(2,1)}), bf16[32,16,256]{2,1,0:T(8,128)(2,1)S(1)}, u32[]{:S(2)}, u32[]{:S(2)}) %all-to-all-start.2) | async-done | bytes 262176 | tf_op jit(solution)/shard_map/all_to_all | solution.py:31
  101.4 2.5 %convolution_bitcast_fusion = f32[4096,256]{0,1:T(8,128)S(1)} fusion(bf16[256,4096]{1,0:T(8,128)(2,1)} %all-gather.2.cloned.1.call-done, bf16[512,256]{1,0:T(8,128)(2,1)S(1)} %bitcast.115, s32[]{:T(128)S(6)} %select_n.111), kind=kOutput, calls=%fused_computation | convolution fusion | flops 536870912 | bytes 6422532 | tf_op jit(solution)/shard_map/dot_general | solution.py:86
  103.9 0.7 convolution_bitcast_fusion.1
  104.6 1.5 copy-done.14
  106.1 1.2 convolution_convert_fusion
  107.3 1.6 collective-permute-start
  108.9 6.8 %collective-permute-done = f32[4096,256]{0,1:T(8,128)S(1)} collective-permute-done((f32[4096,256]{0,1:T(8,128)S(1)}, f32[4096,256]{0,1:T(8,128)S(1)}, u32[]{:S(2)}, u32[]{:S(2)}) %collective-permute-start) | collective-permute-done | bytes 4194336 | tf_op jit(solution)/shard_map/ppermute | solution.py:93
  115.7 2.6 %add_multiply_fusion = f32[4096,256]{0,1:T(8,128)} fusion(f32[4096,256]{0,1:T(8,128)S(1)} %convolution_bitcast_fusion.1, f32[4096,256]{0,1:T(8,128)S(1)} %collective-permute-done), kind=kLoop, calls=%fused_computation.12 | loop fusion | flops 2097152 | bytes 12582912 | tf_op jit(solution)/shard_map/mul | solution.py:93
  118.4 15.2 %all_to_all.36 = bf16[32,16,256]{2,1,0:T(8,128)(2,1)S(1)} all-to-all(bf16[32,16,256]{2,1,0:T(8,128)(2,1)S(1)} %bitcast.118), channel_id=1, replica_groups=mesh['seq'=32,'tp'=8] {'seq'}, dimensions={0} | all-to-all | bytes 524288 | tf_op jit(solution)/shard_map/all_to_all | solution.py:24
  133.7 2.9 %fusion.38 = f32[16,256,128]{1,2,0:T(8,128)S(1)} fusion(bf16[32,16,256]{2,1,0:T(8,128)(2,1)S(1)} %all_to_all.36, bf16[32,16,256]{2,1,0:T(8,128)(2,1)} %all-to-all-done.1, f32[64,32]{0,1:T(8,128)S(1)} %get-tuple-element.50, f32[64,32]{0,1:T(8,128)S(1)} %copy-done.9), kind=kOutput, calls=%fused_computation.63 | convolution fusion | flops 201723904 | bytes 2637824 | tf_op jit(solution)/shard_map/kp,fpcr->fkcr/dot_general | solution.py:57
  136.5 1.2 copy.90
  138.2 3.5 %fusion.16 = f32[1,64,16,512]{3,2,1,0:T(8,128)S(1)} fusion(f32[1,64,16,256]{3,2,1,0:T(8,128)S(1)} %get-tuple-element.37, f32[1,64,16,256]{3,2,1,0:T(8,128)S(1)} %get-tuple-element.36, f32[256,256]{1,0:T(8,128)S(1)} %get-tuple-element.55, f32[256,256]{1,0:T(8,128)S(1)} %get-tuple-element.54, f32[256,256]{1,0:T(8,128)S(1)} %fusion.56), kind=kOutput, calls=%fused_computation.30 | convolution fusion | flops 3222536192 | bytes 4980736 | tf_op jit(solution)/shard_map/fkcr,rq->fkcq/dot_general | solution.py:65
  141.7 0.7 multiply_add_fusion.3
  143.0 9.1 %fusion.4 = f32[2,64,16,512]{3,1,2,0:T(8,128)S(1)} fusion(f32[2,64,16,512]{3,2,1,0:T(8,128)S(1)} %maximum_maximum_fusion, f32[256,256]{1,0:T(8,128)S(1)} %get-tuple-element.55, f32[256,256]{1,0:T(8,128)S(1)} %fusion.56, f32[256,256]{1,0:T(8,128)S(1)} %get-tuple-element.54), kind=kOutput, calls=%fused_computation.8 | convolution fusion | flops 6443237376 | bytes 9175040 | tf_op jit(solution)/shard_map/fkcq,qr->fkcr/dot_general | solution.py:70
  152.9 2.4 %fusion.18 = f32[2,32,16,256]{3,1,2,0:T(8,128)S(1)} fusion(f32[2,64,16,256]{3,1,2,0:T(8,128)S(1)} %get-tuple-element.31, f32[2,64,16,256]{3,1,2,0:T(8,128)S(1)} %get-tuple-element.30, f32[32,64]{1,0:T(8,128)S(1)} %copy-done.10, f32[32,64]{1,0:T(8,128)S(1)} %copy-done.11), kind=kOutput, calls=%fused_computation.36 | convolution fusion | flops 403709952 | bytes 5259264 | tf_op jit(solution)/shard_map/pk,fkcr->fpcr/dot_general | solution.py:77
  157.0 5.3 %all-to-all-start.6 = ((f32[32,1,16]{2,1,0:T(1,128)}), f32[32,1,16]{2,1,0:T(1,128)S(1)}, u32[]{:S(2)}, u32[]{:S(2)}) async-start(f32[32,1,16]{2,1,0:T(1,128)} %broadcast_in_dim.2), calls=%async_computation.6 | async-start | bytes 32768 | tf_op jit(solution)/shard_map/all_to_all | solution.py:155
  162.3 1.1 copy.54
  163.4 6.8 %all-to-all-done.6 = f32[32,1,16]{2,1,0:T(1,128)S(1)} async-done(((f32[32,1,16]{2,1,0:T(1,128)}), f32[32,1,16]{2,1,0:T(1,128)S(1)}, u32[]{:S(2)}, u32[]{:S(2)}) %all-to-all-start.6) | async-done | bytes 2080 | tf_op jit(solution)/shard_map/all_to_all | solution.py:155
  170.2 4.3 %all-to-all-start.5 = ((f32[32,16,256]{2,1,0:T(8,128)}), f32[32,16,256]{2,1,0:T(8,128)S(1)}, u32[]{:S(2)}, u32[]{:S(2)}) async-start(f32[32,16,256]{2,1,0:T(8,128)} %copy.54), calls=%async_computation.5 | async-start | bytes 1048576 | tf_op jit(solution)/shard_map/all_to_all | solution.py:31
  174.5 1.1 slice.155
  175.8 1.1 copy.52
  176.9 18.4 %all-to-all-done.5 = f32[32,16,256]{2,1,0:T(8,128)S(1)} async-done(((f32[32,16,256]{2,1,0:T(8,128)}), f32[32,16,256]{2,1,0:T(8,128)S(1)}, u32[]{:S(2)}, u32[]{:S(2)}) %all-to-all-start.5) | async-done | bytes 524320 | tf_op jit(solution)/shard_map/all_to_all | solution.py:31
  195.3 5.5 %all-to-all-start.4 = ((bf16[2,32,16,256]{3,2,0,1:T(8,128)(2,1)}), bf16[2,32,16,256]{3,2,0,1:T(8,128)(2,1)S(1)}, u32[]{:S(2)}, u32[]{:S(2)}) async-start(bf16[2,32,16,256]{3,2,0,1:T(8,128)(2,1)} %copy.52), calls=%async_computation.4 | async-start | bytes 1048576 | tf_op jit(solution)/shard_map/all_to_all | solution.py:31
  201.5 1.0 copy.57
  202.5 14.8 %all-to-all-done.4 = bf16[2,32,16,256]{3,2,0,1:T(8,128)(2,1)S(1)} async-done(((bf16[2,32,16,256]{3,2,0,1:T(8,128)(2,1)}), bf16[2,32,16,256]{3,2,0,1:T(8,128)(2,1)S(1)}, u32[]{:S(2)}, u32[]{:S(2)}) %all-to-all-start.4) | async-done | bytes 524320 | tf_op jit(solution)/shard_map/all_to_all | solution.py:31
  217.4 1.0 constant_dynamic-slice_fusion.1
  218.4 2.2 collective-permute-start.1
  220.6 0.8 copy.55
  221.4 0.8 copy.56
  222.3 0.8 copy.58
  (63 shorter events, 8.6 us)
Async XLA Ops:
  9.6 12.9 %copy-start.7 = (bf16[256,512]{1,0:T(8,128)(2,1)S(1)}, bf16[256,512]{1,0:T(8,128)(2,1)}, u32[]{:S(2)}) copy-start(bf16[256,512]{1,0:T(8,128)(2,1)} %param.7) | copy-start | bytes 786436
  10.7 37.5 %all-to-all-start = ((f32[2,32,16,256]{3,2,0,1:T(8,128)}), f32[2,32,16,256]{3,2,0,1:T(8,128)S(1)}, u32[]{:S(2)}, u32[]{:S(2)}) async-start(f32[2,32,16,256]{3,2,0,1:T(8,128)} %copy.39), calls=%async_computation | async-start | bytes 2097152 | tf_op jit(solution)/shard_map/all_to_all | solution.py:24
  21.8 79.6 %all-gather.2.cloned.1.call-start = ((), (), s32[]{:S(2)}) async-start(), calls=%async_computation.8 | async-start | bytes 2359296 | tf_op jit(solution)/shard_map/all_gather | solution.py:113
  24.1 31.0 %copy-start.12 = (f32[16]{0:T(128)}, f32[16]{0:T(128)S(1)}, u32[]{:S(2)}) copy-start(f32[16]{0:T(128)S(1)} %dynamic-slice_negate_fusion) | copy-start | bytes 196
  24.2 31.3 %copy-start.8 = (f32[64,32]{0,1:T(8,128)}, f32[64,32]{0,1:T(8,128)S(1)}, u32[]{:S(2)}) copy-start(f32[64,32]{0,1:T(8,128)S(1)} %get-tuple-element.51) | copy-start | bytes 24580
  27.3 28.2 %copy-start.5 = (f32[32,256]{1,0:T(8,128)}, f32[32,256]{1,0:T(8,128)S(1)}, u32[]{:S(2)}) copy-start(f32[32,256]{1,0:T(8,128)S(1)} %convert_multiply_fusion.4) | copy-start | bytes 98308
  48.3 27.7 %all-to-all-start.1 = ((bf16[32,16,256]{2,1,0:T(8,128)(2,1)}), bf16[32,16,256]{2,1,0:T(8,128)(2,1)}, u32[]{:S(2)}, u32[]{:S(2)}) async-start(bf16[32,16,256]{2,1,0:T(8,128)(2,1)} %bitcast.9), calls=%async_computation.1 | async-start | bytes 524288 | tf_op jit(solution)/shard_map/all_to_all | solution.py:24
  69.9 2.0 copy-start
  81.1 20.3 %all-to-all-start.2 = ((bf16[32,16,256]{2,1,0:T(8,128)(2,1)}), bf16[32,16,256]{2,1,0:T(8,128)(2,1)S(1)}, u32[]{:S(2)}, u32[]{:S(2)}) async-start(bf16[32,16,256]{2,1,0:T(8,128)(2,1)} %copy.46), calls=%async_computation.2 | async-start | bytes 524288 | tf_op jit(solution)/shard_map/all_to_all | solution.py:31
  89.5 127.8 %reduce-scatter.2.cloned.1.call-start = ((), (), s32[]{:S(2)}) async-start(), calls=%async_computation.9 | async-start | bytes 4456448 | tf_op jit(solution)/shard_map/reduce_scatter | solution.py:94
  101.4 2.5 %copy-start.2 = (bf16[256,4096]{1,0:T(8,128)(2,1)S(1)}, bf16[256,4096]{1,0:T(8,128)(2,1)}, u32[]{:S(2)}) copy-start(bf16[256,4096]{1,0:T(8,128)(2,1)} %all-gather.2.cloned.1.call-done) | copy-start | bytes 6291460
  103.9 2.2 copy-start.14
  107.3 8.4 %collective-permute-start = (f32[4096,256]{0,1:T(8,128)S(1)}, f32[4096,256]{0,1:T(8,128)S(1)}, u32[]{:S(2)}, u32[]{:S(2)}) collective-permute-start(f32[4096,256]{0,1:T(8,128)S(1)} %convolution_bitcast_fusion), channel_id=1, source_target_pairs={{0,8},{8,0},{16,24},{24,16},{32,40},{40,32},{48,56},{56,48},{64,72... | collective-permute-start | bytes 12582920 | tf_op jit(solution)/shard_map/ppermute | solution.py:93
  118.3 15.4 %copy-start.9 = (f32[64,32]{0,1:T(8,128)S(1)}, f32[64,32]{0,1:T(8,128)}, u32[]{:S(2)}) copy-start(f32[64,32]{0,1:T(8,128)} %copy-done.8) | copy-start | bytes 24580
  138.2 3.5 %copy-start.1 = (f32[2,64,16,512]{3,2,1,0:T(8,128)S(1)}, f32[2,64,16,512]{3,2,1,0:T(8,128)}, u32[]{:S(2)}) copy-start(f32[2,64,16,512]{3,2,1,0:T(8,128)} %copy-done) | copy-start | bytes 12582916
  152.1 0.7 copy-start.10
  152.2 0.7 copy-start.11
  152.9 2.5 %copy-start.6 = (f32[32,256]{1,0:T(8,128)S(1)}, f32[32,256]{1,0:T(8,128)}, u32[]{:S(2)}) copy-start(f32[32,256]{1,0:T(8,128)} %copy-done.5) | copy-start | bytes 98308
  152.9 2.5 %copy-start.13 = (f32[16]{0:T(128)S(1)}, f32[16]{0:T(128)}, u32[]{:S(2)}) copy-start(f32[16]{0:T(128)} %copy-done.12) | copy-start | bytes 196
  155.4 1.0 copy-start.4
  155.4 20.3 %copy-start.3 = (f32[32,16,256]{2,0,1:T(8,128)S(1)}, f32[32,16,256]{2,0,1:T(8,128)}, u32[]{:S(2)}) copy-start(f32[32,16,256]{2,0,1:T(8,128)} %get-tuple-element.49) | copy-start | bytes 1572868
  157.0 13.2 %all-to-all-start.6 = ((f32[32,1,16]{2,1,0:T(1,128)}), f32[32,1,16]{2,1,0:T(1,128)S(1)}, u32[]{:S(2)}, u32[]{:S(2)}) async-start(f32[32,1,16]{2,1,0:T(1,128)} %broadcast_in_dim.2), calls=%async_computation.6 | async-start | bytes 32768 | tf_op jit(solution)/shard_map/all_to_all | solution.py:155
  170.2 25.1 %all-to-all-start.5 = ((f32[32,16,256]{2,1,0:T(8,128)}), f32[32,16,256]{2,1,0:T(8,128)S(1)}, u32[]{:S(2)}, u32[]{:S(2)}) async-start(f32[32,16,256]{2,1,0:T(8,128)} %copy.54), calls=%async_computation.5 | async-start | bytes 1048576 | tf_op jit(solution)/shard_map/all_to_all | solution.py:31
  195.3 22.0 %all-to-all-start.4 = ((bf16[2,32,16,256]{3,2,0,1:T(8,128)(2,1)}), bf16[2,32,16,256]{3,2,0,1:T(8,128)(2,1)S(1)}, u32[]{:S(2)}, u32[]{:S(2)}) async-start(bf16[2,32,16,256]{3,2,0,1:T(8,128)(2,1)} %copy.52), calls=%async_computation.4 | async-start | bytes 1048576 | tf_op jit(solution)/shard_map/all_to_all | solution.py:31
  218.4 3.9 %collective-permute-start.1 = (f32[128,256]{0,1:T(8,128)S(1)}, f32[128,256]{0,1:T(8,128)S(1)}, u32[]{:S(2)}, u32[]{:S(2)}) collective-permute-start(f32[128,256]{0,1:T(8,128)S(1)} %get-tuple-element.47), channel_id=1, source_target_pairs={{0,8},{8,0},{16,24},{24,16},{32,40},{40,32},{48,56},{56,48},{64,72... | collective-permute-start | bytes 393224 | tf_op jit(solution)/shard_map/ppermute | solution.py:98
Sparse Core Ops, SparseCore 0:
  25.1 62.3 all-gather.1
  118.4 77.6 reduce-scatter.1
where the time goes:
time: 235 us; the launch traced here: 230 us
  waiting for transfers between devices  80.3 us (34%)
  starting transfers between devices  44.9 us (19%)
  matrix products  43.2 us (18%)
  local copies, waits for them, and re-layouts  19.6 us (8%)
  blocking collectives  15.2 us (6%)
  between operations  14.8 us (6%)
  other arithmetic  12.2 us (5%)
    all_to_all x3, waiting for transfers between devices, to_tokens(): lax.all_to_all(block, 'seq', split_axis=nd, concat_axis=nd, tiled=True)  45.1 us
    all_to_all x2, waiting for transfers between devices, to_channels(): lax.all_to_all(split, 'seq', split_axis=nd, concat_axis=nd, tiled=True)  20.9 us
    all_to_all x3, starting transfers between devices, to_tokens(): lax.all_to_all(block, 'seq', split_axis=nd, concat_axis=nd, tiled=True)  18.2 us
    all_to_all x2, starting transfers between devices, to_channels(): lax.all_to_all(split, 'seq', split_axis=nd, concat_axis=nd, tiled=True)  17.5 us
    all_to_all x1, blocking collectives, to_channels(): lax.all_to_all(split, 'seq', split_axis=nd, concat_axis=nd, tiled=True)  15.2 us
    dot_general x2, matrix products, forward(): out = jnp.einsum('fkcr,rq->fkcq', z, self.fwd_inner, precision=HIGHEST)  13.1 us
    dot_general x2, matrix products, inverse_real(): u = jnp.einsum('fkcq,qr->fkcr', z, self.inv_inner, precision=HIGHEST)  12.6 us
    unnamed x38, local copies, waits for them, and re-layouts  10.6 us
  transfers between devices with their start and end apart: 10, of which 6 were waited for; matrix products, arithmetic and copies ran while one was open for 26% of the time, Pallas kernels for 0%

commit v1 on v0

--- a/solution.py
+++ b/solution.py
@@ -150,10 +150,15 @@
     decay_part = jnp.sum(position * kernel_grad * kernel, axis=(0, 2))
 
     back = to_tokens(jnp.stack([d_values, d_gate]), parts)
-    d_filt = to_tokens(d_filt_c, parts)
-    spread = jnp.broadcast_to(decay_part[None, :], (parts, sub))
-    gathered = lax.all_to_all(spread, "seq", split_axis=0, concat_axis=0, tiled=True)
-    decay_grad = -norm_scale * gathered.reshape(width)
+    lanes = 128
+    slab = jnp.zeros((parts, sub, lanes), jnp.float32).at[:, :, 0].set(
+        jnp.broadcast_to(decay_part[None, :], (parts, sub))
+    )
+    moved = lax.all_to_all(
+        jnp.concatenate([d_filt_c, slab], axis=2), "seq", split_axis=0, concat_axis=0, tiled=True
+    )
+    d_filt = jnp.transpose(moved[:, :, :tok_rows].reshape(width, tok_rows))
+    decay_grad = -norm_scale * moved[:, :, tok_rows].reshape(width)
     return (back[0], back[1], d_filt, decay_grad, d_out_weight)
 
 

time: 235 us -> 232 us (0.987)
  the two profiles are of different devices: /device:TPU:1 before, /device:TPU:17 now
where the time goes in v1:
time: 232 us; the launch traced here: 228 us
  waiting for transfers between devices  66.4 us (29%)
  starting transfers between devices  57.2 us (25%)
  matrix products  43.7 us (19%)
  local copies, waits for them, and re-layouts  18 us (8%)
  blocking collectives  15.3 us (7%)
  between operations  14.8 us (6%)
  other arithmetic  12.3 us (5%)
    all_to_all x2, waiting for transfers between devices, to_tokens(): lax.all_to_all(block, 'seq', split_axis=nd, concat_axis=nd, tiled=True)  32.6 us
    all_to_all x2, waiting for transfers between devices, to_channels(): lax.all_to_all(split, 'seq', split_axis=nd, concat_axis=nd, tiled=True)  20.9 us
    ppermute x1, starting transfers between devices, pair_reduce(): got = lax.ppermute(given, 'seq', pairs)  20.8 us
    all_to_all x2, starting transfers between devices, to_channels(): lax.all_to_all(split, 'seq', split_axis=nd, concat_axis=nd, tiled=True)  16.7 us
    all_to_all x1, blocking collectives, to_channels(): lax.all_to_all(split, 'seq', split_axis=nd, concat_axis=nd, tiled=True)  15.3 us
    all_to_all x2, starting transfers between devices, to_tokens(): lax.all_to_all(block, 'seq', split_axis=nd, concat_axis=nd, tiled=True)  13.8 us
    dot_general x2, matrix products, forward(): out = jnp.einsum('fkcr,rq->fkcq', z, self.fwd_inner, precision=HIGHEST)  13.1 us
    dot_general x2, matrix products, inverse_real(): u = jnp.einsum('fkcq,qr->fkcr', z, self.inv_inner, precision=HIGHEST)  13.1 us
  transfers between devices with their start and end apart: 9, of which 5 were waited for; matrix products, arithmetic and copies ran while one was open for 26% of the time, Pallas kernels for 0%

profile of v1, /device:TPU:17, one launch (start us, length us, event | category | flops | bytes accessed | tf_op | source)
XLA Modules:
  0.0 227.7 jit_solution(11838164056365802458)
XLA Ops:
  7.2 1.1 copy.38
  8.3 1.2 copy.39
  9.6 1.1 copy.40
  10.7 10.2 %all-to-all-start = ((f32[2,32,16,256]{3,2,0,1:T(8,128)}), f32[2,32,16,256]{3,2,0,1:T(8,128)S(1)}, u32[]{:S(2)}, u32[]{:S(2)}) async-start(f32[2,32,16,256]{3,2,0,1:T(8,128)} %copy.40), calls=%async_computation | async-start | bytes 2097152 | tf_op jit(solution)/shard_map/all_to_all | solution.py:24
  21.0 0.7 all-gather.2.cloned.1.call-update
  21.7 0.8 copy.44
  22.6 0.8 dynamic-slice_negate_fusion
  23.4 0.7 sine_negate_fusion
  24.4 1.0 fusion.57
  25.4 1.0 fusion.55
  26.5 20.9 %all-to-all-done = f32[2,32,16,256]{3,2,0,1:T(8,128)S(1)} async-done(((f32[2,32,16,256]{3,2,0,1:T(8,128)}), f32[2,32,16,256]{3,2,0,1:T(8,128)S(1)}, u32[]{:S(2)}, u32[]{:S(2)}) %all-to-all-start) | async-done | bytes 1048608 | tf_op jit(solution)/shard_map/all_to_all | solution.py:24
  47.4 6.5 %all-to-all-start.1 = ((bf16[32,16,256]{2,1,0:T(8,128)(2,1)}), bf16[32,16,256]{2,1,0:T(8,128)(2,1)}, u32[]{:S(2)}, u32[]{:S(2)}) async-start(bf16[32,16,256]{2,1,0:T(8,128)(2,1)} %bitcast.9), calls=%async_computation.1 | async-start | bytes 524288 | tf_op jit(solution)/shard_map/all_to_all | solution.py:24
  54.7 3.6 %convolution_bitcast_fusion.2 = f32[2,128,16,256]{3,1,2,0:T(8,128)S(1)} fusion(f32[1,32,16,256]{3,1,2,0:T(8,128)S(1)} %multiply_multiply_fusion.1, f32[1,32,16,256]{3,1,2,0:T(8,128)S(1)} %copy.66, f32[64,32]{0,1:T(8,128)S(1)} %get-tuple-element.62, f32[64,32]{0,1:T(8,128)S(1)} %get-tuple-element.63), kind=kOutput, calls=%fused_computation.13 | convolution fusion | flops 402919424 | bytes 5259264 | tf_op jit(solution)/shard_map/kp,fpcr->fkcr/dot_general | solution.py:57
  59.4 9.7 %fusion.6 = f32[2,64,16,512]{3,2,1,0:T(8,128)S(1)} fusion(f32[2,64,16,512]{3,1,2,0:T(8,128)S(1)} %pad_maximum_fusion, f32[256,256]{1,0:T(8,128)S(1)} %get-tuple-element.67, f32[256,256]{1,0:T(8,128)S(1)} %get-tuple-element.66, f32[256,256]{1,0:T(8,128)S(1)} %fusion.57), kind=kOutput, calls=%fused_computation.10 | convolution fusion | flops 6443237376 | bytes 9175040 | tf_op jit(solution)/shard_map/fkcr,rq->fkcq/dot_general | solution.py:65
  69.5 1.6 copy-done
  71.1 3.5 %fusion.17 = f32[1,64,16,512]{3,2,1,0:T(8,128)S(1)} fusion(f32[1,64,16,256]{3,2,1,0:T(8,128)S(1)} %get-tuple-element.47, f32[1,64,16,256]{3,2,1,0:T(8,128)S(1)} %get-tuple-element.46, f32[256,256]{1,0:T(8,128)S(1)} %get-tuple-element.67, f32[256,256]{1,0:T(8,128)S(1)} %fusion.57, f32[256,256]{1,0:T(8,128)S(1)} %get-tuple-element.66), kind=kOutput, calls=%fused_computation.31 | convolution fusion | flops 3222536192 | bytes 4980736 | tf_op jit(solution)/shard_map/fkcq,qr->fkcr/dot_general | solution.py:70
  75.1 4.2 %fusion.37 = (bf16[32,16,256]{2,0,1:T(8,128)(2,1)S(1)}, f32[32,16,256]{2,0,1:T(8,128)}) fusion(bf16[32,16,256]{2,1,0:T(8,128)(2,1)} %all-to-all-done.1, f32[32,64]{1,0:T(8,128)} %get-tuple-element.68, f32[32,64]{1,0:T(8,128)} %get-tuple-element.69, f32[128,16,256]{2,1,0:T(8,128)S(1)} %maximum_bitcast_fusion.2), kind=kOutput, calls=%fused_computation.64 | convolution fusion | flops 201728000 | bytes 3162112 | tf_op jit(solution)/shard_map/pk,fkcr->fpcr/dot_general | solution.py:77
  79.4 0.9 copy.47
  80.2 8.4 %all-to-all-start.2 = ((bf16[32,16,256]{2,1,0:T(8,128)(2,1)}), bf16[32,16,256]{2,1,0:T(8,128)(2,1)S(1)}, u32[]{:S(2)}, u32[]{:S(2)}) async-start(bf16[32,16,256]{2,1,0:T(8,128)(2,1)} %copy.47), calls=%async_computation.2 | async-start | bytes 524288 | tf_op jit(solution)/shard_map/all_to_all | solution.py:31
  88.7 11.8 %all-to-all-done.2 = bf16[32,16,256]{2,1,0:T(8,128)(2,1)S(1)} async-done(((bf16[32,16,256]{2,1,0:T(8,128)(2,1)}), bf16[32,16,256]{2,1,0:T(8,128)(2,1)S(1)}, u32[]{:S(2)}, u32[]{:S(2)}) %all-to-all-start.2) | async-done | bytes 262176 | tf_op jit(solution)/shard_map/all_to_all | solution.py:31
  100.6 2.5 %convolution_bitcast_fusion = f32[4096,256]{0,1:T(8,128)S(1)} fusion(bf16[256,4096]{1,0:T(8,128)(2,1)} %all-gather.2.cloned.1.call-done, bf16[512,256]{1,0:T(8,128)(2,1)S(1)} %bitcast.115, s32[]{:T(128)S(6)} %select_n.111), kind=kOutput, calls=%fused_computation | convolution fusion | flops 536870912 | bytes 6422532 | tf_op jit(solution)/shard_map/dot_general | solution.py:86
  103.1 0.7 convolution_bitcast_fusion.1
  103.8 1.5 copy-done.13
  105.2 1.2 convolution_convert_fusion
  106.5 1.6 collective-permute-start
  108.1 6.8 %collective-permute-done = f32[4096,256]{0,1:T(8,128)S(1)} collective-permute-done((f32[4096,256]{0,1:T(8,128)S(1)}, f32[4096,256]{0,1:T(8,128)S(1)}, u32[]{:S(2)}, u32[]{:S(2)}) %collective-permute-start) | collective-permute-done | bytes 4194336 | tf_op jit(solution)/shard_map/ppermute | solution.py:93
  114.9 2.6 %add_multiply_fusion = f32[4096,256]{0,1:T(8,128)} fusion(f32[4096,256]{0,1:T(8,128)S(1)} %convolution_bitcast_fusion.1, f32[4096,256]{0,1:T(8,128)S(1)} %collective-permute-done), kind=kLoop, calls=%fused_computation.12 | loop fusion | flops 2097152 | bytes 12582912 | tf_op jit(solution)/shard_map/mul | solution.py:93
  117.6 15.3 %all_to_all.30 = bf16[32,16,256]{2,1,0:T(8,128)(2,1)S(1)} all-to-all(bf16[32,16,256]{2,1,0:T(8,128)(2,1)S(1)} %bitcast.118), channel_id=1, replica_groups=mesh['seq'=32,'tp'=8] {'seq'}, dimensions={0} | all-to-all | bytes 524288 | tf_op jit(solution)/shard_map/all_to_all | solution.py:24
  132.9 2.9 %fusion.38 = f32[16,256,128]{1,2,0:T(8,128)S(1)} fusion(bf16[32,16,256]{2,1,0:T(8,128)(2,1)S(1)} %all_to_all.30, bf16[32,16,256]{2,1,0:T(8,128)(2,1)} %all-to-all-done.1, f32[64,32]{0,1:T(8,128)S(1)} %get-tuple-element.62, f32[64,32]{0,1:T(8,128)S(1)} %copy-done.8), kind=kOutput, calls=%fused_computation.65 | convolution fusion | flops 201723904 | bytes 2637824 | tf_op jit(solution)/shard_map/kp,fpcr->fkcr/dot_general | solution.py:57
  135.8 1.2 copy.91
  137.4 3.5 %fusion.16 = f32[1,64,16,512]{3,2,1,0:T(8,128)S(1)} fusion(f32[1,64,16,256]{3,2,1,0:T(8,128)S(1)} %get-tuple-element.49, f32[1,64,16,256]{3,2,1,0:T(8,128)S(1)} %get-tuple-element.48, f32[256,256]{1,0:T(8,128)S(1)} %get-tuple-element.67, f32[256,256]{1,0:T(8,128)S(1)} %get-tuple-element.66, f32[256,256]{1,0:T(8,128)S(1)} %fusion.57), kind=kOutput, calls=%fused_computation.30 | convolution fusion | flops 3222536192 | bytes 4980736 | tf_op jit(solution)/shard_map/fkcr,rq->fkcq/dot_general | solution.py:65
  140.9 0.7 multiply_add_fusion.3
  142.3 9.6 %fusion.4 = f32[2,64,16,512]{3,1,2,0:T(8,128)S(1)} fusion(f32[2,64,16,512]{3,2,1,0:T(8,128)S(1)} %maximum_maximum_fusion, f32[256,256]{1,0:T(8,128)S(1)} %get-tuple-element.67, f32[256,256]{1,0:T(8,128)S(1)} %fusion.57, f32[256,256]{1,0:T(8,128)S(1)} %get-tuple-element.66), kind=kOutput, calls=%fused_computation.8 | convolution fusion | flops 6443237376 | bytes 9175040 | tf_op jit(solution)/shard_map/fkcq,qr->fkcr/dot_general | solution.py:70
  151.9 0.6 multiply_subtract_fusion
  152.7 2.4 %fusion.18 = f32[2,32,16,256]{3,1,2,0:T(8,128)S(1)} fusion(f32[2,64,16,256]{3,1,2,0:T(8,128)S(1)} %get-tuple-element.43, f32[2,64,16,256]{3,1,2,0:T(8,128)S(1)} %get-tuple-element.42, f32[32,64]{1,0:T(8,128)S(1)} %copy-done.9, f32[32,64]{1,0:T(8,128)S(1)} %copy-done.10), kind=kOutput, calls=%fused_computation.36 | convolution fusion | flops 403709952 | bytes 5259264 | tf_op jit(solution)/shard_map/pk,fkcr->fpcr/dot_general | solution.py:77
  155.4 1.1 copy.53
  156.4 5.3 %all-to-all-start.4 = ((bf16[2,32,16,256]{3,2,0,1:T(8,128)(2,1)}), bf16[2,32,16,256]{3,2,0,1:T(8,128)(2,1)S(1)}, u32[]{:S(2)}, u32[]{:S(2)}) async-start(bf16[2,32,16,256]{3,2,0,1:T(8,128)(2,1)} %copy.53), calls=%async_computation.4 | async-start | bytes 1048576 | tf_op jit(solution)/shard_map/all_to_all | solution.py:31
  162.5 1.4 copy.55
  163.9 20.8 %all-to-all-done.4 = bf16[2,32,16,256]{3,2,0,1:T(8,128)(2,1)S(1)} async-done(((bf16[2,32,16,256]{3,2,0,1:T(8,128)(2,1)}), bf16[2,32,16,256]{3,2,0,1:T(8,128)(2,1)S(1)}, u32[]{:S(2)}, u32[]{:S(2)}) %all-to-all-start.4) | async-done | bytes 524320 | tf_op jit(solution)/shard_map/all_to_all | solution.py:31
  184.7 4.3 %all-to-all-start.5 = ((f32[32,16,384]{2,1,0:T(8,128)}), f32[32,16,384]{2,1,0:T(8,128)S(1)}, u32[]{:S(2)}, u32[]{:S(2)}) async-start(f32[32,16,384]{2,1,0:T(8,128)} %copy.55), calls=%async_computation.5 | async-start | bytes 1572864 | tf_op jit(solution)/shard_map/all_to_all | solution.py:157
  189.1 5.4 %reduce-scatter.2.cloned.1.call-done = f32[256,256]{0,1:T(8,128)} async-done(((f32[4096,256]{0,1:T(8,128)}), f32[256,256]{0,1:T(8,128)}) %reduce-scatter.2.cloned.1.call-update) | async-done | bytes 262160 | tf_op jit(solution)/shard_map/reduce_scatter | solution.py:94
  194.4 1.0 constant_dynamic-slice_fusion.1
  195.4 20.8 %collective-permute-start.1 = (f32[128,256]{0,1:T(8,128)S(1)}, f32[128,256]{0,1:T(8,128)S(1)}, u32[]{:S(2)}, u32[]{:S(2)}) collective-permute-start(f32[128,256]{0,1:T(8,128)S(1)} %get-tuple-element.59), channel_id=1, source_target_pairs={{0,8},{8,0},{16,24},{24,16},{32,40},{40,32},{48,56},{56,48},{64,72... | collective-permute-start | bytes 393224 | tf_op jit(solution)/shard_map/ppermute | solution.py:98
  216.2 0.8 copy.56
  217.1 0.8 copy.57
  218.0 1.0 copy.58
  219.1 0.7 mul.632
  219.8 0.8 copy.59
  (61 shorter events, 6.0 us)
Async XLA Ops:
  9.6 12.1 %copy-start.6 = (bf16[256,512]{1,0:T(8,128)(2,1)S(1)}, bf16[256,512]{1,0:T(8,128)(2,1)}, u32[]{:S(2)}) copy-start(bf16[256,512]{1,0:T(8,128)(2,1)} %param.9) | copy-start | bytes 786436
  10.7 36.7 %all-to-all-start = ((f32[2,32,16,256]{3,2,0,1:T(8,128)}), f32[2,32,16,256]{3,2,0,1:T(8,128)S(1)}, u32[]{:S(2)}, u32[]{:S(2)}) async-start(f32[2,32,16,256]{3,2,0,1:T(8,128)} %copy.40), calls=%async_computation | async-start | bytes 2097152 | tf_op jit(solution)/shard_map/all_to_all | solution.py:24
  21.0 79.6 %all-gather.2.cloned.1.call-start = ((), (), s32[]{:S(2)}) async-start(), calls=%async_computation.7 | async-start | bytes 2359296 | tf_op jit(solution)/shard_map/all_gather | solution.py:113
  23.3 31.0 %copy-start.11 = (f32[16]{0:T(128)}, f32[16]{0:T(128)S(1)}, u32[]{:S(2)}) copy-start(f32[16]{0:T(128)S(1)} %dynamic-slice_negate_fusion) | copy-start | bytes 196
  23.4 31.3 %copy-start.7 = (f32[64,32]{0,1:T(8,128)}, f32[64,32]{0,1:T(8,128)S(1)}, u32[]{:S(2)}) copy-start(f32[64,32]{0,1:T(8,128)S(1)} %get-tuple-element.63) | copy-start | bytes 24580
  26.5 28.2 %copy-start.4 = (f32[32,256]{1,0:T(8,128)}, f32[32,256]{1,0:T(8,128)S(1)}, u32[]{:S(2)}) copy-start(f32[32,256]{1,0:T(8,128)S(1)} %convert_multiply_fusion.4) | copy-start | bytes 98308
  47.4 27.7 %all-to-all-start.1 = ((bf16[32,16,256]{2,1,0:T(8,128)(2,1)}), bf16[32,16,256]{2,1,0:T(8,128)(2,1)}, u32[]{:S(2)}, u32[]{:S(2)}) async-start(bf16[32,16,256]{2,1,0:T(8,128)(2,1)} %bitcast.9), calls=%async_computation.1 | async-start | bytes 524288 | tf_op jit(solution)/shard_map/all_to_all | solution.py:24
  69.1 2.0 copy-start
  80.2 20.3 %all-to-all-start.2 = ((bf16[32,16,256]{2,1,0:T(8,128)(2,1)}), bf16[32,16,256]{2,1,0:T(8,128)(2,1)S(1)}, u32[]{:S(2)}, u32[]{:S(2)}) async-start(bf16[32,16,256]{2,1,0:T(8,128)(2,1)} %copy.47), calls=%async_computation.2 | async-start | bytes 524288 | tf_op jit(solution)/shard_map/all_to_all | solution.py:31
  88.7 105.8 %reduce-scatter.2.cloned.1.call-start = ((), (), s32[]{:S(2)}) async-start(), calls=%async_computation.8 | async-start | bytes 4456448 | tf_op jit(solution)/shard_map/reduce_scatter | solution.py:94
  100.6 2.5 %copy-start.2 = (bf16[256,4096]{1,0:T(8,128)(2,1)S(1)}, bf16[256,4096]{1,0:T(8,128)(2,1)}, u32[]{:S(2)}) copy-start(bf16[256,4096]{1,0:T(8,128)(2,1)} %all-gather.2.cloned.1.call-done) | copy-start | bytes 6291460
  103.0 2.2 copy-start.13
  106.5 8.4 %collective-permute-start = (f32[4096,256]{0,1:T(8,128)S(1)}, f32[4096,256]{0,1:T(8,128)S(1)}, u32[]{:S(2)}, u32[]{:S(2)}) collective-permute-start(f32[4096,256]{0,1:T(8,128)S(1)} %convolution_bitcast_fusion), channel_id=1, source_target_pairs={{0,8},{8,0},{16,24},{24,16},{32,40},{40,32},{48,56},{56,48},{64,72... | collective-permute-start | bytes 12582920 | tf_op jit(solution)/shard_map/ppermute | solution.py:93
  117.4 15.5 %copy-start.8 = (f32[64,32]{0,1:T(8,128)S(1)}, f32[64,32]{0,1:T(8,128)}, u32[]{:S(2)}) copy-start(f32[64,32]{0,1:T(8,128)} %copy-done.7) | copy-start | bytes 24580
  137.4 3.5 %copy-start.1 = (f32[2,64,16,512]{3,2,1,0:T(8,128)S(1)}, f32[2,64,16,512]{3,2,1,0:T(8,128)}, u32[]{:S(2)}) copy-start(f32[2,64,16,512]{3,2,1,0:T(8,128)} %copy-done) | copy-start | bytes 12582916
  151.9 0.7 copy-start.9
  151.9 0.7 copy-start.10
  152.7 2.5 %copy-start.3 = (f32[32,16,256]{2,0,1:T(8,128)S(1)}, f32[32,16,256]{2,0,1:T(8,128)}, u32[]{:S(2)}) copy-start(f32[32,16,256]{2,0,1:T(8,128)} %get-tuple-element.61) | copy-start | bytes 1572868
  155.1 6.7 %copy-start.5 = (f32[32,256]{1,0:T(8,128)S(1)}, f32[32,256]{1,0:T(8,128)}, u32[]{:S(2)}) copy-start(f32[32,256]{1,0:T(8,128)} %copy-done.4) | copy-start | bytes 98308
  155.1 6.7 %copy-start.12 = (f32[16]{0:T(128)S(1)}, f32[16]{0:T(128)}, u32[]{:S(2)}) copy-start(f32[16]{0:T(128)} %copy-done.11) | copy-start | bytes 196
  156.4 28.3 %all-to-all-start.4 = ((bf16[2,32,16,256]{3,2,0,1:T(8,128)(2,1)}), bf16[2,32,16,256]{3,2,0,1:T(8,128)(2,1)S(1)}, u32[]{:S(2)}, u32[]{:S(2)}) async-start(bf16[2,32,16,256]{3,2,0,1:T(8,128)(2,1)} %copy.53), calls=%async_computation.4 | async-start | bytes 1048576 | tf_op jit(solution)/shard_map/all_to_all | solution.py:31
  184.7 33.2 %all-to-all-start.5 = ((f32[32,16,384]{2,1,0:T(8,128)}), f32[32,16,384]{2,1,0:T(8,128)S(1)}, u32[]{:S(2)}, u32[]{:S(2)}) async-start(f32[32,16,384]{2,1,0:T(8,128)} %copy.55), calls=%async_computation.5 | async-start | bytes 1572864 | tf_op jit(solution)/shard_map/all_to_all | solution.py:157
  195.4 24.4 %collective-permute-start.1 = (f32[128,256]{0,1:T(8,128)S(1)}, f32[128,256]{0,1:T(8,128)S(1)}, u32[]{:S(2)}, u32[]{:S(2)}) collective-permute-start(f32[128,256]{0,1:T(8,128)S(1)} %get-tuple-element.59), channel_id=1, source_target_pairs={{0,8},{8,0},{16,24},{24,16},{32,40},{40,32},{48,56},{56,48},{64,72... | collective-permute-start | bytes 393224 | tf_op jit(solution)/shard_map/ppermute | solution.py:98
Sparse Core Ops, SparseCore 0:
  24.3 60.6 all-gather.1
  117.6 76.8 reduce-scatter.1

commit v2 on v1

--- a/solution.py
+++ b/solution.py
@@ -90,7 +90,8 @@
 def pair_reduce(keep, send, core, parts, norm_scale):
     pairs = [(i, i ^ 1) for i in range(parts)]
     groups = [list(range(0, parts, 2)), list(range(1, parts, 2))]
-    pair_sum = (keep + lax.ppermute(send, "seq", pairs)) * norm_scale
+    sent = lax.ppermute((send * norm_scale).astype(jnp.bfloat16), "seq", pairs)
+    pair_sum = keep * norm_scale + sent.astype(jnp.float32)
     rows = lax.psum_scatter(pair_sum, "seq", scatter_dimension=0, tiled=True, axis_index_groups=groups)
     block = rows.shape[0] // 2
     own = lax.dynamic_slice_in_dim(rows, core * block, block, axis=0)

time: 232 us -> 230 us (level)
  waiting for transfers between devices: 66.4 us -> 63.3 us
    ppermute x1, waiting for transfers between devices: 6.79 us -> 3.79 us  [pair_reduce(): sent = lax.ppermute((send * norm_scale).astype(jnp.bfloat16), 'seq', pairs)]
    add x0 -> x1, other arithmetic: none -> 2.67 us  [pair_reduce(): pair_sum = keep * norm_scale + sent.astype(jnp.float32)]
    mul x1 -> x0, other arithmetic: 2.56 us -> none  [pair_reduce(): pair_sum = (keep + lax.ppermute(send, 'seq', pairs)) * norm_scale]
where the time goes in v2:
time: 230 us; the launch traced here: 225 us
  waiting for transfers between devices  63.3 us (28%)
  starting transfers between devices  57.3 us (25%)
  matrix products  43.7 us (19%)
  local copies, waits for them, and re-layouts  18 us (8%)
  blocking collectives  15.3 us (7%)
  between operations  14.8 us (6%)
  other arithmetic  12.8 us (6%)
    all_to_all x2, waiting for transfers between devices, to_tokens(): lax.all_to_all(block, 'seq', split_axis=nd, concat_axis=nd, tiled=True)  32.6 us
    all_to_all x2, waiting for transfers between devices, to_channels(): lax.all_to_all(split, 'seq', split_axis=nd, concat_axis=nd, tiled=True)  20.9 us
    ppermute x1, starting transfers between devices, pair_reduce(): got = lax.ppermute(given, 'seq', pairs)  20.8 us
    all_to_all x2, starting transfers between devices, to_channels(): lax.all_to_all(split, 'seq', split_axis=nd, concat_axis=nd, tiled=True)  16.7 us
    all_to_all x1, blocking collectives, to_channels(): lax.all_to_all(split, 'seq', split_axis=nd, concat_axis=nd, tiled=True)  15.3 us
    all_to_all x2, starting transfers between devices, to_tokens(): lax.all_to_all(block, 'seq', split_axis=nd, concat_axis=nd, tiled=True)  13.8 us
    dot_general x2, matrix products, forward(): out = jnp.einsum('fkcr,rq->fkcq', z, self.fwd_inner, precision=HIGHEST)  13.1 us
    dot_general x2, matrix products, inverse_real(): u = jnp.einsum('fkcq,qr->fkcr', z, self.inv_inner, precision=HIGHEST)  13.1 us
  transfers between devices with their start and end apart: 9, of which 5 were waited for; matrix products, arithmetic and copies ran while one was open for 26% of the time, Pallas kernels for 0%

profile of v2, /device:TPU:17, one launch (start us, length us, event | category | flops | bytes accessed | tf_op | source)
XLA Modules:
  0.0 225.1 jit_solution(18288733731371287279)
XLA Ops:
  7.2 1.1 copy.38
  8.3 1.2 copy.39
  9.6 1.1 copy.40
  10.7 10.2 %all-to-all-start = ((f32[2,32,16,256]{3,2,0,1:T(8,128)}), f32[2,32,16,256]{3,2,0,1:T(8,128)S(1)}, u32[]{:S(2)}, u32[]{:S(2)}) async-start(f32[2,32,16,256]{3,2,0,1:T(8,128)} %copy.40), calls=%async_computation | async-start | bytes 2097152 | tf_op jit(solution)/shard_map/all_to_all | solution.py:24
  21.0 0.7 all-gather.2.cloned.1.call-update
  21.7 0.8 copy.44
  22.6 0.8 dynamic-slice_negate_fusion
  23.4 0.7 sine_negate_fusion
  24.4 1.0 fusion.57
  25.4 1.0 fusion.55
  26.5 20.9 %all-to-all-done = f32[2,32,16,256]{3,2,0,1:T(8,128)S(1)} async-done(((f32[2,32,16,256]{3,2,0,1:T(8,128)}), f32[2,32,16,256]{3,2,0,1:T(8,128)S(1)}, u32[]{:S(2)}, u32[]{:S(2)}) %all-to-all-start) | async-done | bytes 1048608 | tf_op jit(solution)/shard_map/all_to_all | solution.py:24
  47.4 6.5 %all-to-all-start.1 = ((bf16[32,16,256]{2,1,0:T(8,128)(2,1)}), bf16[32,16,256]{2,1,0:T(8,128)(2,1)}, u32[]{:S(2)}, u32[]{:S(2)}) async-start(bf16[32,16,256]{2,1,0:T(8,128)(2,1)} %bitcast.9), calls=%async_computation.1 | async-start | bytes 524288 | tf_op jit(solution)/shard_map/all_to_all | solution.py:24
  54.7 3.6 %convolution_bitcast_fusion.2 = f32[2,128,16,256]{3,1,2,0:T(8,128)S(1)} fusion(f32[1,32,16,256]{3,1,2,0:T(8,128)S(1)} %multiply_multiply_fusion.1, f32[1,32,16,256]{3,1,2,0:T(8,128)S(1)} %copy.66, f32[64,32]{0,1:T(8,128)S(1)} %get-tuple-element.62, f32[64,32]{0,1:T(8,128)S(1)} %get-tuple-element.63), kind=kOutput, calls=%fused_computation.14 | convolution fusion | flops 402919424 | bytes 5259264 | tf_op jit(solution)/shard_map/kp,fpcr->fkcr/dot_general | solution.py:57
  59.4 9.7 %fusion.6 = f32[2,64,16,512]{3,2,1,0:T(8,128)S(1)} fusion(f32[2,64,16,512]{3,1,2,0:T(8,128)S(1)} %pad_maximum_fusion, f32[256,256]{1,0:T(8,128)S(1)} %get-tuple-element.67, f32[256,256]{1,0:T(8,128)S(1)} %get-tuple-element.66, f32[256,256]{1,0:T(8,128)S(1)} %fusion.57), kind=kOutput, calls=%fused_computation.10 | convolution fusion | flops 6443237376 | bytes 9175040 | tf_op jit(solution)/shard_map/fkcr,rq->fkcq/dot_general | solution.py:65
  69.5 1.6 copy-done
  71.1 3.5 %fusion.17 = f32[1,64,16,512]{3,2,1,0:T(8,128)S(1)} fusion(f32[1,64,16,256]{3,2,1,0:T(8,128)S(1)} %get-tuple-element.47, f32[1,64,16,256]{3,2,1,0:T(8,128)S(1)} %get-tuple-element.46, f32[256,256]{1,0:T(8,128)S(1)} %get-tuple-element.67, f32[256,256]{1,0:T(8,128)S(1)} %fusion.57, f32[256,256]{1,0:T(8,128)S(1)} %get-tuple-element.66), kind=kOutput, calls=%fused_computation.32 | convolution fusion | flops 3222536192 | bytes 4980736 | tf_op jit(solution)/shard_map/fkcq,qr->fkcr/dot_general | solution.py:70
  75.1 4.2 %fusion.37 = (bf16[32,16,256]{2,0,1:T(8,128)(2,1)S(1)}, f32[32,16,256]{2,0,1:T(8,128)}) fusion(bf16[32,16,256]{2,1,0:T(8,128)(2,1)} %all-to-all-done.1, f32[32,64]{1,0:T(8,128)} %get-tuple-element.68, f32[32,64]{1,0:T(8,128)} %get-tuple-element.69, f32[128,16,256]{2,1,0:T(8,128)S(1)} %maximum_bitcast_fusion.2), kind=kOutput, calls=%fused_computation.65 | convolution fusion | flops 201728000 | bytes 3162112 | tf_op jit(solution)/shard_map/pk,fkcr->fpcr/dot_general | solution.py:77
  79.4 0.9 copy.47
  80.2 8.4 %all-to-all-start.2 = ((bf16[32,16,256]{2,1,0:T(8,128)(2,1)}), bf16[32,16,256]{2,1,0:T(8,128)(2,1)S(1)}, u32[]{:S(2)}, u32[]{:S(2)}) async-start(bf16[32,16,256]{2,1,0:T(8,128)(2,1)} %copy.47), calls=%async_computation.2 | async-start | bytes 524288 | tf_op jit(solution)/shard_map/all_to_all | solution.py:31
  88.7 11.8 %all-to-all-done.2 = bf16[32,16,256]{2,1,0:T(8,128)(2,1)S(1)} async-done(((bf16[32,16,256]{2,1,0:T(8,128)(2,1)}), bf16[32,16,256]{2,1,0:T(8,128)(2,1)S(1)}, u32[]{:S(2)}, u32[]{:S(2)}) %all-to-all-start.2) | async-done | bytes 262176 | tf_op jit(solution)/shard_map/all_to_all | solution.py:31
  100.6 2.5 %convolution_bitcast_fusion = f32[4096,256]{0,1:T(8,128)S(1)} fusion(bf16[256,4096]{1,0:T(8,128)(2,1)} %all-gather.2.cloned.1.call-done, bf16[512,256]{1,0:T(8,128)(2,1)S(1)} %bitcast.115, s32[]{:T(128)S(6)} %select_n.111), kind=kOutput, calls=%fused_computation | convolution fusion | flops 536870912 | bytes 6422532 | tf_op jit(solution)/shard_map/dot_general | solution.py:86
  103.1 0.7 convolution_bitcast_fusion.1
  103.8 1.5 copy-done.13
  105.2 1.2 convolution_convert_fusion
  106.9 1.6 collective-permute-start
  108.5 3.8 %collective-permute-done = bf16[4096,256]{0,1:T(8,128)(2,1)S(1)} collective-permute-done((bf16[4096,256]{0,1:T(8,128)(2,1)S(1)}, bf16[4096,256]{0,1:T(8,128)(2,1)S(1)}, u32[]{:S(2)}, u32[]{:S(2)}) %collective-permute-start) | collective-permute-done | bytes 2097184 | tf_op jit(solution)/shard_map/ppermute | solution.py:93
  112.2 2.7 %convert_add_fusion = f32[4096,256]{0,1:T(8,128)} fusion(bf16[4096,256]{0,1:T(8,128)(2,1)S(1)} %collective-permute-done, f32[4096,256]{0,1:T(8,128)S(1)} %convolution_bitcast_fusion.1), kind=kLoop, calls=%fused_computation.12 | loop fusion | flops 3145728 | bytes 10485760 | tf_op jit(solution)/shard_map/add | solution.py:94
  115.1 15.3 %all_to_all.30 = bf16[32,16,256]{2,1,0:T(8,128)(2,1)S(1)} all-to-all(bf16[32,16,256]{2,1,0:T(8,128)(2,1)S(1)} %bitcast.118), channel_id=1, replica_groups=mesh['seq'=32,'tp'=8] {'seq'}, dimensions={0} | all-to-all | bytes 524288 | tf_op jit(solution)/shard_map/all_to_all | solution.py:24
  130.4 2.9 %fusion.38 = f32[16,256,128]{1,2,0:T(8,128)S(1)} fusion(bf16[32,16,256]{2,1,0:T(8,128)(2,1)S(1)} %all_to_all.30, bf16[32,16,256]{2,1,0:T(8,128)(2,1)} %all-to-all-done.1, f32[64,32]{0,1:T(8,128)S(1)} %get-tuple-element.62, f32[64,32]{0,1:T(8,128)S(1)} %copy-done.8), kind=kOutput, calls=%fused_computation.66 | convolution fusion | flops 201723904 | bytes 2637824 | tf_op jit(solution)/shard_map/kp,fpcr->fkcr/dot_general | solution.py:57
  133.3 1.2 copy.91
  134.9 3.5 %fusion.16 = f32[1,64,16,512]{3,2,1,0:T(8,128)S(1)} fusion(f32[1,64,16,256]{3,2,1,0:T(8,128)S(1)} %get-tuple-element.49, f32[1,64,16,256]{3,2,1,0:T(8,128)S(1)} %get-tuple-element.48, f32[256,256]{1,0:T(8,128)S(1)} %get-tuple-element.67, f32[256,256]{1,0:T(8,128)S(1)} %get-tuple-element.66, f32[256,256]{1,0:T(8,128)S(1)} %fusion.57), kind=kOutput, calls=%fused_computation.31 | convolution fusion | flops 3222536192 | bytes 4980736 | tf_op jit(solution)/shard_map/fkcr,rq->fkcq/dot_general | solution.py:65
  138.4 0.7 multiply_add_fusion.3
  139.8 9.6 %fusion.4 = f32[2,64,16,512]{3,1,2,0:T(8,128)S(1)} fusion(f32[2,64,16,512]{3,2,1,0:T(8,128)S(1)} %maximum_maximum_fusion, f32[256,256]{1,0:T(8,128)S(1)} %get-tuple-element.67, f32[256,256]{1,0:T(8,128)S(1)} %fusion.57, f32[256,256]{1,0:T(8,128)S(1)} %get-tuple-element.66), kind=kOutput, calls=%fused_computation.8 | convolution fusion | flops 6443237376 | bytes 9175040 | tf_op jit(solution)/shard_map/fkcq,qr->fkcr/dot_general | solution.py:70
  149.4 0.6 multiply_subtract_fusion
  150.2 2.4 %fusion.18 = f32[2,32,16,256]{3,1,2,0:T(8,128)S(1)} fusion(f32[2,64,16,256]{3,1,2,0:T(8,128)S(1)} %get-tuple-element.43, f32[2,64,16,256]{3,1,2,0:T(8,128)S(1)} %get-tuple-element.42, f32[32,64]{1,0:T(8,128)S(1)} %copy-done.9, f32[32,64]{1,0:T(8,128)S(1)} %copy-done.10), kind=kOutput, calls=%fused_computation.37 | convolution fusion | flops 403709952 | bytes 5259264 | tf_op jit(solution)/shard_map/pk,fkcr->fpcr/dot_general | solution.py:77
  152.9 1.1 copy.53
  153.9 5.3 %all-to-all-start.4 = ((bf16[2,32,16,256]{3,2,0,1:T(8,128)(2,1)}), bf16[2,32,16,256]{3,2,0,1:T(8,128)(2,1)S(1)}, u32[]{:S(2)}, u32[]{:S(2)}) async-start(bf16[2,32,16,256]{3,2,0,1:T(8,128)(2,1)} %copy.53), calls=%async_computation.4 | async-start | bytes 1048576 | tf_op jit(solution)/shard_map/all_to_all | solution.py:31
  160.0 1.4 copy.55
  161.4 20.8 %all-to-all-done.4 = bf16[2,32,16,256]{3,2,0,1:T(8,128)(2,1)S(1)} async-done(((bf16[2,32,16,256]{3,2,0,1:T(8,128)(2,1)}), bf16[2,32,16,256]{3,2,0,1:T(8,128)(2,1)S(1)}, u32[]{:S(2)}, u32[]{:S(2)}) %all-to-all-start.4) | async-done | bytes 524320 | tf_op jit(solution)/shard_map/all_to_all | solution.py:31
  182.2 4.3 %all-to-all-start.5 = ((f32[32,16,384]{2,1,0:T(8,128)}), f32[32,16,384]{2,1,0:T(8,128)S(1)}, u32[]{:S(2)}, u32[]{:S(2)}) async-start(f32[32,16,384]{2,1,0:T(8,128)} %copy.55), calls=%async_computation.5 | async-start | bytes 1572864 | tf_op jit(solution)/shard_map/all_to_all | solution.py:158
  186.5 5.2 %reduce-scatter.2.cloned.1.call-done = f32[256,256]{0,1:T(8,128)} async-done(((f32[4096,256]{0,1:T(8,128)}), f32[256,256]{0,1:T(8,128)}) %reduce-scatter.2.cloned.1.call-update) | async-done | bytes 262160 | tf_op jit(solution)/shard_map/reduce_scatter | solution.py:95
  191.8 1.0 constant_dynamic-slice_fusion.1
  192.8 20.8 %collective-permute-start.1 = (f32[128,256]{0,1:T(8,128)S(1)}, f32[128,256]{0,1:T(8,128)S(1)}, u32[]{:S(2)}, u32[]{:S(2)}) collective-permute-start(f32[128,256]{0,1:T(8,128)S(1)} %get-tuple-element.59), channel_id=1, source_target_pairs={{0,8},{8,0},{16,24},{24,16},{32,40},{40,32},{48,56},{56,48},{64,72... | collective-permute-start | bytes 393224 | tf_op jit(solution)/shard_map/ppermute | solution.py:99
  213.7 0.8 copy.56
  214.5 0.8 copy.57
  215.4 1.0 copy.58
  216.6 0.7 mul.632
  217.2 0.8 copy.59
  (62 shorter events, 6.3 us)
Async XLA Ops:
  9.6 12.1 %copy-start.6 = (bf16[256,512]{1,0:T(8,128)(2,1)S(1)}, bf16[256,512]{1,0:T(8,128)(2,1)}, u32[]{:S(2)}) copy-start(bf16[256,512]{1,0:T(8,128)(2,1)} %param.9) | copy-start | bytes 786436
  10.7 36.7 %all-to-all-start = ((f32[2,32,16,256]{3,2,0,1:T(8,128)}), f32[2,32,16,256]{3,2,0,1:T(8,128)S(1)}, u32[]{:S(2)}, u32[]{:S(2)}) async-start(f32[2,32,16,256]{3,2,0,1:T(8,128)} %copy.40), calls=%async_computation | async-start | bytes 2097152 | tf_op jit(solution)/shard_map/all_to_all | solution.py:24
  21.0 79.6 %all-gather.2.cloned.1.call-start = ((), (), s32[]{:S(2)}) async-start(), calls=%async_computation.7 | async-start | bytes 2359296 | tf_op jit(solution)/shard_map/all_gather | solution.py:114
  23.3 31.0 %copy-start.11 = (f32[16]{0:T(128)}, f32[16]{0:T(128)S(1)}, u32[]{:S(2)}) copy-start(f32[16]{0:T(128)S(1)} %dynamic-slice_negate_fusion) | copy-start | bytes 196
  23.4 31.3 %copy-start.7 = (f32[64,32]{0,1:T(8,128)}, f32[64,32]{0,1:T(8,128)S(1)}, u32[]{:S(2)}) copy-start(f32[64,32]{0,1:T(8,128)S(1)} %get-tuple-element.63) | copy-start | bytes 24580
  26.5 28.2 %copy-start.4 = (f32[32,256]{1,0:T(8,128)}, f32[32,256]{1,0:T(8,128)S(1)}, u32[]{:S(2)}) copy-start(f32[32,256]{1,0:T(8,128)S(1)} %convert_multiply_fusion.4) | copy-start | bytes 98308
  47.4 27.7 %all-to-all-start.1 = ((bf16[32,16,256]{2,1,0:T(8,128)(2,1)}), bf16[32,16,256]{2,1,0:T(8,128)(2,1)}, u32[]{:S(2)}, u32[]{:S(2)}) async-start(bf16[32,16,256]{2,1,0:T(8,128)(2,1)} %bitcast.9), calls=%async_computation.1 | async-start | bytes 524288 | tf_op jit(solution)/shard_map/all_to_all | solution.py:24
  69.1 2.0 copy-start
  80.2 20.3 %all-to-all-start.2 = ((bf16[32,16,256]{2,1,0:T(8,128)(2,1)}), bf16[32,16,256]{2,1,0:T(8,128)(2,1)S(1)}, u32[]{:S(2)}, u32[]{:S(2)}) async-start(bf16[32,16,256]{2,1,0:T(8,128)(2,1)} %copy.47), calls=%async_computation.2 | async-start | bytes 524288 | tf_op jit(solution)/shard_map/all_to_all | solution.py:31
  88.7 103.1 %reduce-scatter.2.cloned.1.call-start = ((), (), s32[]{:S(2)}) async-start(), calls=%async_computation.8 | async-start | bytes 4456448 | tf_op jit(solution)/shard_map/reduce_scatter | solution.py:95
  100.6 2.5 %copy-start.2 = (bf16[256,4096]{1,0:T(8,128)(2,1)S(1)}, bf16[256,4096]{1,0:T(8,128)(2,1)}, u32[]{:S(2)}) copy-start(bf16[256,4096]{1,0:T(8,128)(2,1)} %all-gather.2.cloned.1.call-done) | copy-start | bytes 6291460
  103.0 2.2 copy-start.13
  106.9 5.4 %collective-permute-start = (bf16[4096,256]{0,1:T(8,128)(2,1)S(1)}, bf16[4096,256]{0,1:T(8,128)(2,1)S(1)}, u32[]{:S(2)}, u32[]{:S(2)}) collective-permute-start(bf16[4096,256]{0,1:T(8,128)(2,1)S(1)} %multiply_convert_fusion), channel_id=1, source_target_pairs={{0,8},{8,0},{16,24},{24,16},{32,40},{40,32},{48,56},{56,48},{64,72... | collective-permute-start | bytes 6291464 | tf_op jit(solution)/shard_map/ppermute | solution.py:93
  114.9 15.5 %copy-start.8 = (f32[64,32]{0,1:T(8,128)S(1)}, f32[64,32]{0,1:T(8,128)}, u32[]{:S(2)}) copy-start(f32[64,32]{0,1:T(8,128)} %copy-done.7) | copy-start | bytes 24580
  134.9 3.5 %copy-start.1 = (f32[2,64,16,512]{3,2,1,0:T(8,128)S(1)}, f32[2,64,16,512]{3,2,1,0:T(8,128)}, u32[]{:S(2)}) copy-start(f32[2,64,16,512]{3,2,1,0:T(8,128)} %copy-done) | copy-start | bytes 12582916
  149.4 0.7 copy-start.9
  149.4 0.7 copy-start.10
  150.1 2.5 %copy-start.3 = (f32[32,16,256]{2,0,1:T(8,128)S(1)}, f32[32,16,256]{2,0,1:T(8,128)}, u32[]{:S(2)}) copy-start(f32[32,16,256]{2,0,1:T(8,128)} %get-tuple-element.61) | copy-start | bytes 1572868
  152.6 6.7 %copy-start.5 = (f32[32,256]{1,0:T(8,128)S(1)}, f32[32,256]{1,0:T(8,128)}, u32[]{:S(2)}) copy-start(f32[32,256]{1,0:T(8,128)} %copy-done.4) | copy-start | bytes 98308
  152.6 6.7 %copy-start.12 = (f32[16]{0:T(128)S(1)}, f32[16]{0:T(128)}, u32[]{:S(2)}) copy-start(f32[16]{0:T(128)} %copy-done.11) | copy-start | bytes 196
  153.9 28.3 %all-to-all-start.4 = ((bf16[2,32,16,256]{3,2,0,1:T(8,128)(2,1)}), bf16[2,32,16,256]{3,2,0,1:T(8,128)(2,1)S(1)}, u32[]{:S(2)}, u32[]{:S(2)}) async-start(bf16[2,32,16,256]{3,2,0,1:T(8,128)(2,1)} %copy.53), calls=%async_computation.4 | async-start | bytes 1048576 | tf_op jit(solution)/shard_map/all_to_all | solution.py:31
  182.2 33.1 %all-to-all-start.5 = ((f32[32,16,384]{2,1,0:T(8,128)}), f32[32,16,384]{2,1,0:T(8,128)S(1)}, u32[]{:S(2)}, u32[]{:S(2)}) async-start(f32[32,16,384]{2,1,0:T(8,128)} %copy.55), calls=%async_computation.5 | async-start | bytes 1572864 | tf_op jit(solution)/shard_map/all_to_all | solution.py:158
  192.8 24.4 %collective-permute-start.1 = (f32[128,256]{0,1:T(8,128)S(1)}, f32[128,256]{0,1:T(8,128)S(1)}, u32[]{:S(2)}, u32[]{:S(2)}) collective-permute-start(f32[128,256]{0,1:T(8,128)S(1)} %get-tuple-element.59), channel_id=1, source_target_pairs={{0,8},{8,0},{16,24},{24,16},{32,40},{40,32},{48,56},{56,48},{64,72... | collective-permute-start | bytes 393224 | tf_op jit(solution)/shard_map/ppermute | solution.py:99
Sparse Core Ops, SparseCore 0:
  24.3 60.6 all-gather.1
  115.1 76.6 reduce-scatter.1

commit v3 on v2

--- a/solution.py
+++ b/solution.py
@@ -53,8 +53,8 @@
             [jnp.concatenate([gc, gs], axis=1), jnp.concatenate([-gs, gc], axis=1)], axis=0
         )
 
-    def forward(self, x):
-        y = jnp.einsum("kp,fpcr->fkcr", self.fwd_outer, x, precision=HIGHEST)
+    def forward(self, x, precision=HIGHEST):
+        y = jnp.einsum("kp,fpcr->fkcr", self.fwd_outer, x, precision=precision)
         outer = self.fwd_outer.shape[0] // 2
         yr, yi = y[:, :outer], y[:, outer:]
         tc = self.twid_c[None, :, None, :]
@@ -62,19 +62,19 @@
         zr = yr * tc + yi * ts
         zi = yi * tc - yr * ts
         z = jnp.concatenate([zr, zi], axis=-1)
-        out = jnp.einsum("fkcr,rq->fkcq", z, self.fwd_inner, precision=HIGHEST)
+        out = jnp.einsum("fkcr,rq->fkcq", z, self.fwd_inner, precision=precision)
         return out[..., : self.rows], out[..., self.rows :]
 
-    def inverse_real(self, zr, zi):
+    def inverse_real(self, zr, zi, precision=HIGHEST):
         z = jnp.concatenate([zr, zi], axis=-1)
-        u = jnp.einsum("fkcq,qr->fkcr", z, self.inv_inner, precision=HIGHEST)
+        u = jnp.einsum("fkcq,qr->fkcr", z, self.inv_inner, precision=precision)
         ur, ui = u[..., : self.rows], u[..., self.rows :]
         tc = self.twid_c[None, :, None, :]
         ts = self.twid_s[None, :, None, :]
         vr = ur * tc - ui * ts
         vi = ur * ts + ui * tc
         v = jnp.concatenate([vr, vi], axis=1)
-        return jnp.einsum("pk,fkcr->fpcr", self.inv_outer, v, precision=HIGHEST)
+        return jnp.einsum("pk,fkcr->fpcr", self.inv_outer, v, precision=precision)
 
 
 def pair_products(full_grad, gated_home, core):
@@ -138,11 +138,11 @@
 
     grad_c = to_channels(grad_y, parts).astype(jnp.float32)
     gated_grad = grad_c * gate_c
-    g_r, g_i = dft.forward(gated_grad[None])
+    g_r, g_i = dft.forward(gated_grad[None], lax.Precision.HIGH)
     g_r, g_i = g_r[0], g_i[0]
     prod_r = jnp.stack([k_r * g_r + k_i * g_i, v_r * g_r + v_i * g_i])
     prod_i = jnp.stack([k_r * g_i - k_i * g_r, v_r * g_i - v_i * g_r])
-    conv = dft.inverse_real(prod_r, prod_i)
+    conv = dft.inverse_real(prod_r, prod_i, lax.Precision.HIGH)
     conv_grad, kernel_grad = conv[0], conv[1]
 
     d_values = conv_grad.astype(jnp.bfloat16)

time: 230 us -> 231 us (level)
  the two profiles are of different devices: /device:TPU:17 before, /device:TPU:1 now
where the time goes in v3:
time: 231 us; the launch traced here: 226 us
  waiting for transfers between devices  84 us (36%)
  starting transfers between devices  45.1 us (20%)
  matrix products  35.9 us (16%)
  local copies, waits for them, and re-layouts  18.5 us (8%)
  blocking collectives  15.2 us (7%)
  between operations  14.8 us (6%)
  other arithmetic  12.8 us (6%)
    all_to_all x2, waiting for transfers between devices, to_tokens(): lax.all_to_all(block, 'seq', split_axis=nd, concat_axis=nd, tiled=True)  32 us
    reduce_scatter x1, waiting for transfers between devices, pair_reduce(): lax.psum_scatter(pair_sum, 'seq', scatter_dimension=0, tiled=True, axis_i...  26.7 us
    all_to_all x2, waiting for transfers between devices, to_channels(): lax.all_to_all(split, 'seq', split_axis=nd, concat_axis=nd, tiled=True)  20.9 us
    all_to_all x2, starting transfers between devices, to_channels(): lax.all_to_all(split, 'seq', split_axis=nd, concat_axis=nd, tiled=True)  17.5 us
    all_to_all x1, blocking collectives, to_channels(): lax.all_to_all(split, 'seq', split_axis=nd, concat_axis=nd, tiled=True)  15.2 us
    all_to_all x2, starting transfers between devices, to_tokens(): lax.all_to_all(block, 'seq', split_axis=nd, concat_axis=nd, tiled=True)  13.8 us
    dot_general x2, matrix products, forward(): out = jnp.einsum('fkcr,rq->fkcq', z, self.fwd_inner, precision=precision)  11.5 us
    unnamed x36, local copies, waits for them, and re-layouts  10.6 us
  transfers between devices with their start and end apart: 9, of which 5 were waited for; matrix products, arithmetic and copies ran while one was open for 23% of the time, Pallas kernels for 0%

profile of v3, /device:TPU:1, one launch (start us, length us, event | category | flops | bytes accessed | tf_op | source)
XLA Modules:
  0.0 226.3 jit_solution(13967386286945871362)
XLA Ops:
  7.2 1.1 copy.38
  8.3 1.2 copy.39
  9.6 1.1 copy.40
  10.7 11.0 %all-to-all-start = ((f32[2,32,16,256]{3,2,0,1:T(8,128)}), f32[2,32,16,256]{3,2,0,1:T(8,128)S(1)}, u32[]{:S(2)}, u32[]{:S(2)}) async-start(f32[2,32,16,256]{3,2,0,1:T(8,128)} %copy.40), calls=%async_computation | async-start | bytes 2097152 | tf_op jit(solution)/shard_map/all_to_all | solution.py:24
  21.8 0.7 all-gather.2.cloned.1.call-update
  22.5 0.8 copy.44
  23.4 0.8 dynamic-slice_negate_fusion
  24.2 0.7 sine_negate_fusion
  25.2 1.0 fusion.57
  26.2 1.0 fusion.55
  27.3 20.9 %all-to-all-done = f32[2,32,16,256]{3,2,0,1:T(8,128)S(1)} async-done(((f32[2,32,16,256]{3,2,0,1:T(8,128)}), f32[2,32,16,256]{3,2,0,1:T(8,128)S(1)}, u32[]{:S(2)}, u32[]{:S(2)}) %all-to-all-start) | async-done | bytes 1048608 | tf_op jit(solution)/shard_map/all_to_all | solution.py:24
  48.2 6.5 %all-to-all-start.1 = ((bf16[32,16,256]{2,1,0:T(8,128)(2,1)}), bf16[32,16,256]{2,1,0:T(8,128)(2,1)}, u32[]{:S(2)}, u32[]{:S(2)}) async-start(bf16[32,16,256]{2,1,0:T(8,128)(2,1)} %bitcast.9), calls=%async_computation.1 | async-start | bytes 524288 | tf_op jit(solution)/shard_map/all_to_all | solution.py:24
  55.5 3.6 %convolution_bitcast_fusion.2 = f32[2,128,16,256]{3,1,2,0:T(8,128)S(1)} fusion(f32[1,32,16,256]{3,1,2,0:T(8,128)S(1)} %multiply_multiply_fusion.1, f32[1,32,16,256]{3,1,2,0:T(8,128)S(1)} %copy.66, f32[64,32]{0,1:T(8,128)S(1)} %get-tuple-element.62, f32[64,32]{0,1:T(8,128)S(1)} %get-tuple-element.63), kind=kOutput, calls=%fused_computation.14 | convolution fusion | flops 402919424 | bytes 5259264 | tf_op jit(solution)/shard_map/kp,fpcr->fkcr/dot_general | solution.py:57
  60.2 9.7 %fusion.6 = f32[2,64,16,512]{3,2,1,0:T(8,128)S(1)} fusion(f32[2,64,16,512]{3,1,2,0:T(8,128)S(1)} %pad_maximum_fusion, f32[256,256]{1,0:T(8,128)S(1)} %get-tuple-element.67, f32[256,256]{1,0:T(8,128)S(1)} %get-tuple-element.66, f32[256,256]{1,0:T(8,128)S(1)} %fusion.57), kind=kOutput, calls=%fused_computation.10 | convolution fusion | flops 6443237376 | bytes 9175040 | tf_op jit(solution)/shard_map/fkcr,rq->fkcq/dot_general | solution.py:65
  70.3 1.6 copy-done
  71.9 3.5 %fusion.17 = f32[1,64,16,512]{3,2,1,0:T(8,128)S(1)} fusion(f32[1,64,16,256]{3,2,1,0:T(8,128)S(1)} %get-tuple-element.47, f32[1,64,16,256]{3,2,1,0:T(8,128)S(1)} %get-tuple-element.46, f32[256,256]{1,0:T(8,128)S(1)} %get-tuple-element.67, f32[256,256]{1,0:T(8,128)S(1)} %fusion.57, f32[256,256]{1,0:T(8,128)S(1)} %get-tuple-element.66), kind=kOutput, calls=%fused_computation.32 | convolution fusion | flops 3222536192 | bytes 4980736 | tf_op jit(solution)/shard_map/fkcq,qr->fkcr/dot_general | solution.py:70
  76.0 4.2 %fusion.37 = (bf16[32,16,256]{2,0,1:T(8,128)(2,1)S(1)}, f32[32,16,256]{2,0,1:T(8,128)}) fusion(bf16[32,16,256]{2,1,0:T(8,128)(2,1)} %all-to-all-done.1, f32[32,64]{1,0:T(8,128)} %get-tuple-element.68, f32[32,64]{1,0:T(8,128)} %get-tuple-element.69, f32[128,16,256]{2,1,0:T(8,128)S(1)} %maximum_bitcast_fusion.2), kind=kOutput, calls=%fused_computation.65 | convolution fusion | flops 201728000 | bytes 3162112 | tf_op jit(solution)/shard_map/pk,fkcr->fpcr/dot_general | solution.py:77
  80.2 0.9 copy.47
  81.1 8.4 %all-to-all-start.2 = ((bf16[32,16,256]{2,1,0:T(8,128)(2,1)}), bf16[32,16,256]{2,1,0:T(8,128)(2,1)S(1)}, u32[]{:S(2)}, u32[]{:S(2)}) async-start(bf16[32,16,256]{2,1,0:T(8,128)(2,1)} %copy.47), calls=%async_computation.2 | async-start | bytes 524288 | tf_op jit(solution)/shard_map/all_to_all | solution.py:31
  89.6 11.8 %all-to-all-done.2 = bf16[32,16,256]{2,1,0:T(8,128)(2,1)S(1)} async-done(((bf16[32,16,256]{2,1,0:T(8,128)(2,1)}), bf16[32,16,256]{2,1,0:T(8,128)(2,1)S(1)}, u32[]{:S(2)}, u32[]{:S(2)}) %all-to-all-start.2) | async-done | bytes 262176 | tf_op jit(solution)/shard_map/all_to_all | solution.py:31
  101.4 2.5 %convolution_bitcast_fusion = f32[4096,256]{0,1:T(8,128)S(1)} fusion(bf16[256,4096]{1,0:T(8,128)(2,1)} %all-gather.2.cloned.1.call-done, bf16[512,256]{1,0:T(8,128)(2,1)S(1)} %bitcast.115, s32[]{:T(128)S(6)} %select_n.111), kind=kOutput, calls=%fused_computation | convolution fusion | flops 536870912 | bytes 6422532 | tf_op jit(solution)/shard_map/dot_general | solution.py:86
  103.9 0.7 convolution_bitcast_fusion.1
  104.6 1.5 copy-done.13
  106.1 1.2 convolution_convert_fusion
  107.7 1.6 collective-permute-start
  109.3 3.8 %collective-permute-done = bf16[4096,256]{0,1:T(8,128)(2,1)S(1)} collective-permute-done((bf16[4096,256]{0,1:T(8,128)(2,1)S(1)}, bf16[4096,256]{0,1:T(8,128)(2,1)S(1)}, u32[]{:S(2)}, u32[]{:S(2)}) %collective-permute-start) | collective-permute-done | bytes 2097184 | tf_op jit(solution)/shard_map/ppermute | solution.py:93
  113.1 2.7 %convert_add_fusion = f32[4096,256]{0,1:T(8,128)} fusion(bf16[4096,256]{0,1:T(8,128)(2,1)S(1)} %collective-permute-done, f32[4096,256]{0,1:T(8,128)S(1)} %convolution_bitcast_fusion.1), kind=kLoop, calls=%fused_computation.12 | loop fusion | flops 3145728 | bytes 10485760 | tf_op jit(solution)/shard_map/add | solution.py:94
  115.9 15.2 %all_to_all.30 = bf16[32,16,256]{2,1,0:T(8,128)(2,1)S(1)} all-to-all(bf16[32,16,256]{2,1,0:T(8,128)(2,1)S(1)} %bitcast.118), channel_id=1, replica_groups=mesh['seq'=32,'tp'=8] {'seq'}, dimensions={0} | all-to-all | bytes 524288 | tf_op jit(solution)/shard_map/all_to_all | solution.py:24
  131.2 2.0 fusion.38
  133.2 1.2 copy.91
  134.9 1.8 fusion.16
  137.1 0.7 multiply_add_fusion.3
  138.4 5.5 %fusion.4 = f32[2,64,16,512]{3,1,2,0:T(8,128)S(1)} fusion(f32[2,64,16,512]{3,2,1,0:T(8,128)S(1)} %maximum_maximum_fusion, f32[256,256]{1,0:T(8,128)S(1)} %get-tuple-element.67, f32[256,256]{1,0:T(8,128)S(1)} %fusion.57, f32[256,256]{1,0:T(8,128)S(1)} %get-tuple-element.66), kind=kOutput, calls=%fused_computation.8 | convolution fusion | flops 3222011904 | bytes 9175040 | tf_op jit(solution)/shard_map/fkcq,qr->fkcr/dot_general | solution.py:70
  143.9 0.6 multiply_subtract_fusion
  144.6 1.2 fusion.18
  146.1 1.3 copy.53
  147.4 5.4 %all-to-all-start.4 = ((bf16[2,32,16,256]{3,2,0,1:T(8,128)(2,1)}), bf16[2,32,16,256]{3,2,0,1:T(8,128)(2,1)S(1)}, u32[]{:S(2)}, u32[]{:S(2)}) async-start(bf16[2,32,16,256]{3,2,0,1:T(8,128)(2,1)} %copy.53), calls=%async_computation.4 | async-start | bytes 1048576 | tf_op jit(solution)/shard_map/all_to_all | solution.py:31
  153.5 1.4 copy.55
  154.9 20.1 %all-to-all-done.4 = bf16[2,32,16,256]{3,2,0,1:T(8,128)(2,1)S(1)} async-done(((bf16[2,32,16,256]{3,2,0,1:T(8,128)(2,1)}), bf16[2,32,16,256]{3,2,0,1:T(8,128)(2,1)S(1)}, u32[]{:S(2)}, u32[]{:S(2)}) %all-to-all-start.4) | async-done | bytes 524320 | tf_op jit(solution)/shard_map/all_to_all | solution.py:31
  175.0 4.7 %all-to-all-start.5 = ((f32[32,16,384]{2,1,0:T(8,128)}), f32[32,16,384]{2,1,0:T(8,128)S(1)}, u32[]{:S(2)}, u32[]{:S(2)}) async-start(f32[32,16,384]{2,1,0:T(8,128)} %copy.55), calls=%async_computation.5 | async-start | bytes 1572864 | tf_op jit(solution)/shard_map/all_to_all | solution.py:158
  179.8 26.7 %reduce-scatter.2.cloned.1.call-done = f32[256,256]{0,1:T(8,128)} async-done(((f32[4096,256]{0,1:T(8,128)}), f32[256,256]{0,1:T(8,128)}) %reduce-scatter.2.cloned.1.call-update) | async-done | bytes 262160 | tf_op jit(solution)/shard_map/reduce_scatter | solution.py:95
  206.5 1.0 constant_dynamic-slice_fusion.1
  207.5 7.3 %collective-permute-start.1 = (f32[128,256]{0,1:T(8,128)S(1)}, f32[128,256]{0,1:T(8,128)S(1)}, u32[]{:S(2)}, u32[]{:S(2)}) collective-permute-start(f32[128,256]{0,1:T(8,128)S(1)} %get-tuple-element.59), channel_id=1, source_target_pairs={{0,8},{8,0},{16,24},{24,16},{32,40},{40,32},{48,56},{56,48},{64,72... | collective-permute-start | bytes 393224 | tf_op jit(solution)/shard_map/ppermute | solution.py:99
  214.8 0.8 copy.56
  215.7 0.8 copy.57
  216.6 1.0 copy.58
  217.7 0.7 mul.632
  218.4 0.8 copy.59
  (62 shorter events, 6.7 us)
Async XLA Ops:
  9.6 12.9 %copy-start.6 = (bf16[256,512]{1,0:T(8,128)(2,1)S(1)}, bf16[256,512]{1,0:T(8,128)(2,1)}, u32[]{:S(2)}) copy-start(bf16[256,512]{1,0:T(8,128)(2,1)} %param.9) | copy-start | bytes 786436
  10.7 37.5 %all-to-all-start = ((f32[2,32,16,256]{3,2,0,1:T(8,128)}), f32[2,32,16,256]{3,2,0,1:T(8,128)S(1)}, u32[]{:S(2)}, u32[]{:S(2)}) async-start(f32[2,32,16,256]{3,2,0,1:T(8,128)} %copy.40), calls=%async_computation | async-start | bytes 2097152 | tf_op jit(solution)/shard_map/all_to_all | solution.py:24
  21.8 79.6 %all-gather.2.cloned.1.call-start = ((), (), s32[]{:S(2)}) async-start(), calls=%async_computation.7 | async-start | bytes 2359296 | tf_op jit(solution)/shard_map/all_gather | solution.py:114
  24.1 31.0 %copy-start.11 = (f32[16]{0:T(128)}, f32[16]{0:T(128)S(1)}, u32[]{:S(2)}) copy-start(f32[16]{0:T(128)S(1)} %dynamic-slice_negate_fusion) | copy-start | bytes 196
  24.2 31.3 %copy-start.7 = (f32[64,32]{0,1:T(8,128)}, f32[64,32]{0,1:T(8,128)S(1)}, u32[]{:S(2)}) copy-start(f32[64,32]{0,1:T(8,128)S(1)} %get-tuple-element.63) | copy-start | bytes 24580
  27.3 28.2 %copy-start.4 = (f32[32,256]{1,0:T(8,128)}, f32[32,256]{1,0:T(8,128)S(1)}, u32[]{:S(2)}) copy-start(f32[32,256]{1,0:T(8,128)S(1)} %convert_multiply_fusion.4) | copy-start | bytes 98308
  48.2 27.7 %all-to-all-start.1 = ((bf16[32,16,256]{2,1,0:T(8,128)(2,1)}), bf16[32,16,256]{2,1,0:T(8,128)(2,1)}, u32[]{:S(2)}, u32[]{:S(2)}) async-start(bf16[32,16,256]{2,1,0:T(8,128)(2,1)} %bitcast.9), calls=%async_computation.1 | async-start | bytes 524288 | tf_op jit(solution)/shard_map/all_to_all | solution.py:24
  69.9 2.0 copy-start
  81.1 20.3 %all-to-all-start.2 = ((bf16[32,16,256]{2,1,0:T(8,128)(2,1)}), bf16[32,16,256]{2,1,0:T(8,128)(2,1)S(1)}, u32[]{:S(2)}, u32[]{:S(2)}) async-start(bf16[32,16,256]{2,1,0:T(8,128)(2,1)} %copy.47), calls=%async_computation.2 | async-start | bytes 524288 | tf_op jit(solution)/shard_map/all_to_all | solution.py:31
  89.5 117.0 %reduce-scatter.2.cloned.1.call-start = ((), (), s32[]{:S(2)}) async-start(), calls=%async_computation.8 | async-start | bytes 4456448 | tf_op jit(solution)/shard_map/reduce_scatter | solution.py:95
  101.4 2.5 %copy-start.2 = (bf16[256,4096]{1,0:T(8,128)(2,1)S(1)}, bf16[256,4096]{1,0:T(8,128)(2,1)}, u32[]{:S(2)}) copy-start(bf16[256,4096]{1,0:T(8,128)(2,1)} %all-gather.2.cloned.1.call-done) | copy-start | bytes 6291460
  103.9 2.2 copy-start.13
  107.7 5.4 %collective-permute-start = (bf16[4096,256]{0,1:T(8,128)(2,1)S(1)}, bf16[4096,256]{0,1:T(8,128)(2,1)S(1)}, u32[]{:S(2)}, u32[]{:S(2)}) collective-permute-start(bf16[4096,256]{0,1:T(8,128)(2,1)S(1)} %multiply_convert_fusion), channel_id=1, source_target_pairs={{0,8},{8,0},{16,24},{24,16},{32,40},{40,32},{48,56},{56,48},{64,72... | collective-permute-start | bytes 6291464 | tf_op jit(solution)/shard_map/ppermute | solution.py:93
  115.7 15.4 %copy-start.8 = (f32[64,32]{0,1:T(8,128)S(1)}, f32[64,32]{0,1:T(8,128)}, u32[]{:S(2)}) copy-start(f32[64,32]{0,1:T(8,128)} %copy-done.7) | copy-start | bytes 24580
  134.9 2.2 copy-start.1
  143.9 0.7 copy-start.9
  143.9 0.7 copy-start.10
  144.6 1.3 copy-start.3
  145.9 6.9 %copy-start.5 = (f32[32,256]{1,0:T(8,128)S(1)}, f32[32,256]{1,0:T(8,128)}, u32[]{:S(2)}) copy-start(f32[32,256]{1,0:T(8,128)} %copy-done.4) | copy-start | bytes 98308
  145.9 6.9 %copy-start.12 = (f32[16]{0:T(128)S(1)}, f32[16]{0:T(128)}, u32[]{:S(2)}) copy-start(f32[16]{0:T(128)} %copy-done.11) | copy-start | bytes 196
  147.4 27.6 %all-to-all-start.4 = ((bf16[2,32,16,256]{3,2,0,1:T(8,128)(2,1)}), bf16[2,32,16,256]{3,2,0,1:T(8,128)(2,1)S(1)}, u32[]{:S(2)}, u32[]{:S(2)}) async-start(bf16[2,32,16,256]{3,2,0,1:T(8,128)(2,1)} %copy.53), calls=%async_computation.4 | async-start | bytes 1048576 | tf_op jit(solution)/shard_map/all_to_all | solution.py:31
  175.0 41.5 %all-to-all-start.5 = ((f32[32,16,384]{2,1,0:T(8,128)}), f32[32,16,384]{2,1,0:T(8,128)S(1)}, u32[]{:S(2)}, u32[]{:S(2)}) async-start(f32[32,16,384]{2,1,0:T(8,128)} %copy.55), calls=%async_computation.5 | async-start | bytes 1572864 | tf_op jit(solution)/shard_map/all_to_all | solution.py:158
  207.5 10.9 %collective-permute-start.1 = (f32[128,256]{0,1:T(8,128)S(1)}, f32[128,256]{0,1:T(8,128)S(1)}, u32[]{:S(2)}, u32[]{:S(2)}) collective-permute-start(f32[128,256]{0,1:T(8,128)S(1)} %get-tuple-element.59), channel_id=1, source_target_pairs={{0,8},{8,0},{16,24},{24,16},{32,40},{40,32},{48,56},{56,48},{64,72... | collective-permute-start | bytes 393224 | tf_op jit(solution)/shard_map/ppermute | solution.py:99
Sparse Core Ops, SparseCore 0:
  25.1 62.3 all-gather.1
  115.9 90.5 reduce-scatter.1
